TPU v7x, 32 devices: a whole 2x2x4 slice. The times are simulated.
32 devices in a mesh: case: 4 (over z), span: 2 (over x), vert: 4 (over y, core).
Axes of the slice: x: 2, y: 2, z: 4, core: 2. Of those that a mesh axis runs over, the one named last changes fastest.
Arguments:
- state: float32 [8, 4, 16, 32, 512], P('case', None, 'span', 'vert'), may hold values from -3 to 4.5
- turbine_x: int32 [8, 6], P('case'), may hold values from 128 to 511
- turbine_y: int32 [8, 6], P('case'), may hold values from 0 to 15
- yaw_index: int32 [8], P('case'), may hold values from 0 to 7
Outputs:
- final_state: float32 [8, 4, 16, 32, 512], P('case', None, 'span', 'vert')
All inputs are finite; a program needn't handle non-finite values.
Results may differ from a plain program's by a relative error of at most 0.0003.
Values sent between devices are 32-bit elements; how exact they have to be, the bound alone decides.
No kernel may reach another device: no remote copies, remote signals or barrier semaphores. Data moves between devices by JAX's collectives and lax.ppermute only.
A program may use at most 64 MiB of HBM per device.

v0:
```python
import functools

import jax
import jax.numpy as jnp
from jax import lax
from jax.experimental import pallas as pl
from jax.experimental.pallas import tpu as pltpu
from jax.sharding import PartitionSpec as P


STEPS = 3
DISK = 8
LANES = 128
HALO = 2 * STEPS

U_MEAN = 1.0
VISC = 0.04
THRUST = 0.75
TIME_STEP = 0.1
YAW_STEP = 0.15
HALF = 0.5 * TIME_STEP
SCALES = (HALF * HALF, HALF, HALF, HALF)

ROW0 = 8
STRIP = 16


def flat(blocks):
    _, z, x = blocks.shape[-3:]
    a = blocks.reshape(-1, z, x // LANES, LANES)
    return jnp.swapaxes(a, 1, 2).reshape(-1, LANES)


def unflat(rows, shape):
    _, z, x = shape[-3:]
    a = rows.reshape(-1, x // LANES, z, LANES)
    return jnp.swapaxes(a, 1, 2).reshape(shape)


def away_kernel(dims, state_ref, near_ref, far_ref):
    fields, ry, rz, tiles = dims
    part = ry * tiles * rz
    slot = 1 - lax.axis_index("span")
    even = lax.axis_index("vert") % 2 == 0
    near = jnp.where(even, 0, rz - HALO)
    far = jnp.where(even, HALO, 0)
    for f in range(fields):
        base = (slot * fields + f) * part
        for ref, low, count in ((near_ref, near, HALO), (far_ref, far, rz - HALO)):
            for t in range(tiles):
                for k in range(count):
                    value = state_ref[pl.ds(base + t * rz + low + k, ry, stride=tiles * rz), :]
                    ref[pl.ds(((f * tiles + t) * count + k) * ry, ry), :] = value


def fringe_kernel(dims, held_ref, fringe_ref):
    fields, ry, rz, tiles = dims
    step = tiles * rz
    lane = lax.broadcasted_iota(jnp.int32, (ry, LANES), 1)
    for f in range(fields):
        base = f * ry * step
        strip = jnp.zeros((ry, LANES), jnp.float32)
        for z in range(rz):
            place = f * (rz + 1) + z
            row = base + z
            fringe_ref[pl.ds(place * ry, ry), :] = held_ref[pl.ds(row, ry, stride=step), :]
            after = held_ref[pl.ds(row + rz, ry, stride=step), :]
            before = held_ref[pl.ds(row + (tiles - 1) * rz, ry, stride=step), :]
            both = jnp.where(lane < LANES // 2, after, before)
            both = pltpu.roll(both, (HALO + STRIP * z) % LANES, 1)
            here = (lane >= STRIP * z) & (lane < STRIP * z + 2 * HALO)
            strip = jnp.where(here, both, strip)
        fringe_ref[pl.ds((f * (rz + 1) + rz) * ry, ry), :] = strip


def own_kernel(dims, state_ref, own_ref, near_ref):
    fields, ry, rz, tiles = dims
    size = fields * ry * tiles * rz
    start = lax.axis_index("span") * size
    even = lax.axis_index("vert") % 2 == 0
    near = jnp.where(even, 0, rz - HALO)
    for f in range(fields):
        for t in range(tiles):
            for z in range(rz):
                row = start + (f * ry * tiles + t) * rz + z
                value = state_ref[pl.ds(row, ry, stride=tiles * rz), :]
                own_ref[pl.ds(((f * tiles + t) * rz + z) * ry, ry), :] = value
    for c in range(fields * tiles):
        for k in range(HALO):
            row = pl.multiple_of((c * rz + near + k) * ry, 8)
            near_ref[pl.ds((c * HALO + k) * ry, ry), :] = own_ref[pl.ds(row, ry), :]


def weights_kernel(dims, xs, ys, yaws, trig, wgt):
    ry, tiles, nt, slots = dims
    total_y = 2 * ry
    slot = lax.axis_index("span")
    active = jnp.where(lax.axis_index("case") * slots + slot > 0, 1.0, 0.0)
    lane = lax.broadcasted_iota(jnp.int32, (8, LANES), 1)
    sub = lax.broadcasted_iota(jnp.int32, (8, LANES), 0)
    angle = jnp.full((8, LANES), yaws[slot], jnp.int32).astype(jnp.float32)
    angle = (angle - 3.5) * YAW_STEP
    cos_yaw = jnp.cos(angle)
    sin_yaw = jnp.sin(angle)
    trig[0] = cos_yaw
    trig[1] = sin_yaw
    trig[2] = 0.5 * (1.0 - jnp.cos(jnp.pi * (lane.astype(jnp.float32) + 1.0) / LANES))
    for t in range(1, tiles):
        for g in range(total_y // 8):
            acc = jnp.zeros((8, LANES), jnp.float32)
            y = slot * ry + 8 * g + sub
            for k in range(nt):
                hit = lax.rem(y - ys[slot, k] + 2 * total_y, total_y) < DISK
                hit = hit & (lane + t * LANES == xs[slot, k])
                acc = acc + jnp.where(hit, 1.0, 0.0)
            acc = acc * (active * (2.0 * THRUST))
            wgt[0, 0, t, g] = jnp.zeros((8, LANES), jnp.float32)
            wgt[0, 1, t, g] = jnp.zeros((8, LANES), jnp.float32)
            wgt[1, 0, t, g] = acc * cos_yaw
            wgt[1, 1, t, g] = acc * sin_yaw


class Cells:

    def __init__(self, dims, trig):
        self.dims = fields, ry, rz, tiles = dims
        self.ext = rz + 2 * HALO
        self.rows = self.ext + 2
        self.total_y = 2 * ry
        self.store = 2 * ROW0 + self.total_y
        self.groups = self.total_y // 8
        total_z = rz * lax.axis_size("vert")
        self.slot = lax.axis_index("span")
        vert_at = lax.axis_index("vert")
        z0 = vert_at * rz
        self.even = vert_at % 2 == 0
        self.dlo = jnp.maximum(HALO - z0, 0)
        self.dhi = jnp.minimum(HALO + total_z - z0, self.ext)
        self.gate = HALO + total_z // 2 - z0
        self.one = 1 + jnp.minimum(vert_at, 0)
        self.lane = lax.broadcasted_iota(jnp.int32, (8, LANES), 1)
        self.first_lane = self.lane == 0
        self.last_lane = self.lane == LANES - 1
        self.cos_yaw, self.sin_yaw, self.ramp = trig[0], trig[1], trig[2]

    def put(self, dst, width, f, t, z, group, value):
        start = pl.multiple_of(((f * width + t) * self.rows + z + 1) * self.store, 8)
        dst[pl.ds(start + (ROW0 + 8 * group), 8), :] = value
        if group == 0:
            dst[pl.ds(start + (ROW0 + self.total_y), 1), :] = value[0:1]
        if group == self.groups - 1:
            dst[pl.ds(start + (ROW0 - 1), 1), :] = value[7:8]

    def clear_outside(self, *refs):
        fields, rz = self.dims[0], self.dims[2]
        zero = jnp.zeros((self.store, LANES), jnp.float32)
        for ref, width in refs:
            for z in (HALO - 1, HALO + rz):

                def clear(ref=ref, width=width, z=z):
                    for c in range(fields * width):
                        ref[pl.ds((c * self.rows + z + 1) * self.store, self.store), :] = zero

                pl.when((z < self.dlo) | (z >= self.dhi))(clear)

    def stage(self, src, base, dst, width, k, wgt=None, pq=None, outs=None):
        second = k % 2 == 0
        fields, ry, rz, tiles = self.dims
        rows, store, ext, groups, one = self.rows, self.store, self.ext, self.groups, self.one
        dlo, dhi, gate = self.dlo, self.dhi, self.gate
        cos_yaw, sin_yaw, ramp = self.cos_yaw, self.sin_yaw, self.ramp
        first_lane, last_lane, sides0, sides1 = self.first_lane, self.last_lane, *self.sides

        def at(ref, f, t, g, z, dy=0):
            start = ((f * width + t % width) * rows + z + 1) * store + ROW0 + 8 * g
            start = start + dy * one if dy else pl.multiple_of(start, 8)
            return ref[pl.ds(start, 8), :]

        def beside(f, t, g, side):
            return pl.ds((((f * 2 + side) * width + t) * groups + g) * 8, 8)

        def shift(z, into, t, g):
            for f in range(fields):
                c = at(src, f, t, g, z)
                after = at(src, f, t + 1, g, z)
                before = at(src, f, t - 1, g, z)
                east = pltpu.roll(jnp.where(first_lane, after, c), LANES - 1, 1)
                west = pltpu.roll(jnp.where(last_lane, before, c), 1, 1)
                into[beside(f, t, g, 0), :] = east
                into[beside(f, t, g, 1), :] = west

        def row(z, sides, following):
            if wgt is not None:
                on = jnp.where(z < gate, 1, 0)
            for t in range(width):
                for g in range(groups):
                    shift(z + 1, following, t, g)
                    c = [at(src, f, t, g, z) for f in range(fields)]
                    gx, gy, gz, lap = [], [], [], []
                    for f in range(fields):
                        east = sides[beside(f, t, g, 0), :]
                        west = sides[beside(f, t, g, 1), :]
                        north = at(src, f, t, g, z, dy=1)
                        south = at(src, f, t, g, z, dy=-1)
                        upper = at(src, f, t, g, z + 1)
                        lower = at(src, f, t, g, z - 1)
                        gx.append(east - west)
                        gy.append(north - south)
                        gz.append(upper - lower)
                        around = ((east + west) + (north + south)) + (upper + lower)
                        lap.append(around - 6.0 * c[f])
                    speed = c[1] + HALF * U_MEAN
                    strain = gx[1] * gx[1] + gy[2] * gy[2] + gz[3] * gz[3]
                    strain = strain + gy[1] * gy[1] + gz[1] * gz[1] + 4.0 * HALF * HALF
                    viscous = VISC * (strain * lax.rsqrt(strain))
                    rate = [
                        viscous * lap[f] - (speed * gx[f] + c[2] * gy[f] + c[3] * gz[f])
                        for f in range(fields)
                    ]
                    rate[0] = rate[0] - HALF * HALF * (gx[1] + gy[2] + gz[3])
                    rate[1] = rate[1] - gx[0]
                    rate[2] = rate[2] - gy[0]
                    rate[3] = rate[3] - gz[0]
                    if wgt is not None and t > 0:
                        normal = speed * cos_yaw + c[2] * sin_yaw
                        thrust = normal * jnp.abs(normal)
                        rate[1] = rate[1] - thrust * wgt[on, 0, t, g]
                        rate[2] = rate[2] - thrust * wgt[on, 1, t, g]
                    for f in range(fields):
                        if second:
                            new = 0.5 * ((at(base, f, t, g, z) + c[f]) + rate[f])
                            if pq is not None and t == 0:
                                start = pl.multiple_of((f * 2 * rows + z + 1) * store, 8)
                                new = new + ramp * (pq[pl.ds(start + (ROW0 + 8 * g), 8), :] - new)
                        else:
                            new = c[f] + rate[f]
                        if outs is not None:
                            out = outs[0] if g < groups // 2 else outs[1]
                            start = ((f * tiles + t) * rz + z - HALO) * ry + 8 * (g % (groups // 2))
                            new = new * (1.0 / SCALES[f])
                            out[pl.ds(pl.multiple_of(start, 8), 8), :] = new
                        else:
                            self.put(dst, width, f, t, z, g, new)

        first = jnp.maximum(k, dlo)
        count = jnp.minimum(ext - k, dhi) - first
        first = first - jnp.where(dhi < ext, count & 1, 0)
        for t in range(width):
            for g in range(groups):
                shift(first, sides0, t, g)

        def pair(i, carry):
            z = first + 2 * i
            row(z, sides0, sides1)
            row(z + 1, sides1, sides0)
            return carry

        lax.fori_loop(0, (count + 1) // 2, pair, 0)


def scale_of(f):
    return jnp.where(f == 0, SCALES[0], SCALES[1])


def first_kernel(
    dims, trig, wgt, own, got_near, got_far, out_own, out_got, in_own, in_near, in_far,
    q, m, sides0, sides1,
):
    fields, ry, rz, tiles = dims
    cells = Cells(dims, trig)
    cells.sides = sides0, sides1
    put = cells.put

    def fill(parts):
        def one_field(f, carry):
            for src, held, taken, half, z_dst, count in parts:
                for t in range(tiles):
                    for k in range(count):
                        row = pl.multiple_of(((f * tiles + t) * held + taken + k) * ry, 8)
                        for g in range(ry // 8):
                            value = scale_of(f) * src[pl.ds(row + 8 * g, 8), :]
                            put(q, tiles, f, t, z_dst + k, half * (ry // 8) + g, value)
            return carry

        lax.fori_loop(0, fields, one_field, 0)

    def pick(a, b):
        return jnp.where(cells.even, a, b)

    above = HALO + rz
    rest = rz - HALO
    fill(
        (
            (own, rz, 0, 0, HALO, rz),
            (in_own, rz, pick(0, rest), 0, pick(above, 0), HALO),
            (out_own, HALO, 0, 0, pick(0, above), HALO),
        )
    )
    fill(
        (
            (got_near, HALO, 0, 1, HALO + pick(0, rest), HALO),
            (got_far, rest, 0, 1, HALO + pick(HALO, 0), rest),
            (out_got, HALO, 0, 1, pick(0, above), HALO),
            (in_near, HALO, pick(0, rest), 1, pick(above + rest, 0), HALO - rest),
            (in_far, rest, 0, 1, pick(above, HALO - rest), rest),
        )
    )
    cells.clear_outside((q, tiles), (m, tiles))
    cells.stage(q, None, m, tiles, 1, wgt)
    cells.stage(m, q, q, tiles, 2, wgt)


def rest_kernel(
    dims, trig, wgt, q_in, p_own, p_out, p_in, mine_ref, send_ref, q, m, pq, pm, sides0, sides1
):
    del q_in
    fields, ry, rz, tiles = dims
    cells = Cells(dims, trig)
    cells.sides = sides0, sides1
    put = cells.put

    def fill_fringe(parts):
        def one_field(f, carry):
            for src, taken, half, z_dst, count in parts:
                base = (half * fields + f) * (rz + 1)
                strip = scale_of(f) * src[pl.ds(pl.multiple_of((base + rz) * ry, 8), ry), :]
                for k in range(count):
                    z = taken + k
                    row = pl.multiple_of((base + z) * ry, 8)
                    put(pq, 2, f, 0, z_dst + k, half, scale_of(f) * src[pl.ds(row, ry), :])
                    value = pltpu.roll(strip, 2 * LANES - HALO - STRIP * z, 1)
                    put(pq, 2, f, 1, z_dst + k, half, value)
            return carry

        lax.fori_loop(0, fields, one_field, 0)

    def pick(a, b):
        return jnp.where(cells.even, a, b)

    above = HALO + rz
    rest = rz - HALO
    for half in range(2):
        fill_fringe(
            (
                (p_own, 0, half, HALO, rz),
                (p_out, pick(rest, 0), half, pick(0, above), HALO),
                (p_in, pick(0, rest), half, pick(above, 0), HALO),
            )
        )
    cells.clear_outside((pq, 2), (pm, 2), (m, tiles))
    for step in range(STEPS):
        k = 2 * step + 1
        cells.stage(pq, None, pm, 2, k)
        cells.stage(pm, pq, pq, 2, k + 1)
        if step == 0:

            def relax(z, carry):
                for f in range(fields):
                    for g in range(cells.groups):
                        row = (f * tiles * cells.rows + z + 1) * cells.store + ROW0 + 8 * g
                        source = (f * 2 * cells.rows + z + 1) * cells.store + ROW0 + 8 * g
                        value = q[pl.ds(pl.multiple_of(row, 8), 8), :]
                        value = value + cells.ramp * (pq[pl.ds(pl.multiple_of(source, 8), 8), :] - value)
                        put(q, tiles, f, 0, z, g, value)
                return carry

            low = jnp.maximum(k + 1, cells.dlo)
            lax.fori_loop(low, jnp.minimum(cells.ext - k - 1, cells.dhi), relax, 0)
        else:
            last = (mine_ref, send_ref) if step == STEPS - 1 else None
            cells.stage(q, None, m, tiles, k, wgt)
            cells.stage(m, q, q, tiles, k + 1, wgt, pq, last)


def place_kernel(dims, other, *refs):
    fields, ry, rz, tiles = dims
    src, out_ref, block, sems = refs[0], refs[-3], refs[-2], refs[-1]
    size = ry * tiles * rz
    slot = lax.axis_index("span")
    slot = 1 - slot if other else slot
    copies = []
    for f in range(fields):
        for y in range(ry):
            for t in range(tiles):
                value = src[pl.ds((f * tiles + t) * rz * ry + y, rz, stride=ry), :]
                block[pl.ds(((f * ry + y) * tiles + t) * rz, rz), :] = value
        start = pl.multiple_of((slot * fields + f) * size, 8)
        part = block.at[pl.ds(f * size, size)]
        copies.append(pltpu.make_async_copy(part, out_ref.at[pl.ds(start, size)], sems.at[f]))
        copies[-1].start()
    for copy in copies:
        copy.wait()


def swaps(size):
    inner = [(i, i ^ 1) for i in range(size)]
    outer = [(i, i + 1 if i % 2 else i - 1) for i in range(size)]
    outer = [(i, j) for i, j in outer if 0 <= j < size]
    return inner, outer


def spread(value, axis):
    size = lax.axis_size(axis)
    at = lax.axis_index(axis)
    gap = size // 2
    while gap:
        pairs = [(i, i + gap) for i in range(0, size, 2 * gap)]
        moved = lax.ppermute(value, axis, pairs)
        value = jnp.where(at % (2 * gap) == gap, moved, value)
        gap //= 2
    return value


def body(state, turbine_x, turbine_y, yaw_index):
    slots, fields, ry, rz, x = state.shape
    tiles = x // LANES
    nt = turbine_x.shape[1]
    count = fields * ry * tiles * rz
    near_count = count // rz * HALO
    fringe_count = fields * (rz + 1) * ry
    dims = (fields, ry, rz, tiles)
    inner, outer = swaps(lax.axis_size("vert"))
    across = [(0, 1), (1, 0)]
    smem = pl.BlockSpec(memory_space=pltpu.SMEM)
    vmem = pl.BlockSpec(memory_space=pltpu.VMEM)
    hbm = pl.BlockSpec(memory_space=pl.ANY)
    whole = flat(state)

    def rows_of(n):
        return jax.ShapeDtypeStruct((n, LANES), jnp.float32)

    def block_of(n):
        return pltpu.VMEM((n, LANES), jnp.float32)

    small = pltpu.CompilerParams(vmem_limit_bytes=8 << 20)
    away_near, away_far = pl.pallas_call(
        functools.partial(away_kernel, dims),
        out_shape=[rows_of(near_count), rows_of(count - near_count)],
        in_specs=[vmem],
        out_specs=[vmem] * 2,
        compiler_params=small,
        name="away",
    )(whole)
    fringe = pl.pallas_call(
        functools.partial(fringe_kernel, dims),
        out_shape=rows_of(fringe_count),
        in_specs=[vmem],
        out_specs=vmem,
        compiler_params=small,
        name="fringe",
    )(whole)
    got_near = lax.ppermute(away_near, "span", across)
    got_far = lax.ppermute(away_far, "span", across)
    own, near = pl.pallas_call(
        functools.partial(own_kernel, dims),
        out_shape=[rows_of(count), rows_of(near_count)],
        in_specs=[vmem],
        out_specs=[vmem] * 2,
        compiler_params=small,
        name="own",
    )(whole)
    out_own = lax.ppermute(near, "vert", outer)
    in_own = lax.ppermute(own, "vert", inner)
    fringe = spread(fringe, "case")
    fringe_got = lax.ppermute(fringe, "span", across)
    out_got = lax.ppermute(got_near, "vert", outer)
    in_near = lax.ppermute(got_near, "vert", inner)
    in_far = lax.ppermute(got_far, "vert", inner)
    fringes = [jnp.concatenate([fringe, fringe_got])]
    for pairs in (outer, inner):
        fringes.append(lax.ppermute(fringes[0], "vert", pairs))
    ext = rz + 2 * HALO
    store = 2 * ROW0 + 2 * ry
    size = fields * (ext + 2) * store
    weights = (2, 2, tiles, 2 * ry // 8, 8, LANES)
    sides = [block_of(fields * 2 * tiles * 2 * ry)] * 2
    large = pltpu.CompilerParams(vmem_limit_bytes=20 << 20)
    trig, wgt = pl.pallas_call(
        functools.partial(weights_kernel, (ry, tiles, nt, slots)),
        out_shape=[
            jax.ShapeDtypeStruct((3, 8, LANES), jnp.float32),
            jax.ShapeDtypeStruct(weights, jnp.float32),
        ],
        in_specs=[smem] * 3,
        out_specs=[vmem, vmem],
        compiler_params=small,
        name="weights",
    )(turbine_x, turbine_y, yaw_index)
    q = pl.pallas_call(
        functools.partial(first_kernel, dims),
        out_shape=rows_of(size * tiles),
        in_specs=[vmem] * 10,
        out_specs=vmem,
        scratch_shapes=[block_of(size * tiles)] + sides,
        compiler_params=large,
        name="first",
    )(trig, wgt, own, got_near, got_far, out_own, out_got, in_own, in_near, in_far)
    mine, send, _ = pl.pallas_call(
        functools.partial(rest_kernel, dims),
        out_shape=[rows_of(count)] * 2 + [rows_of(size * tiles)],
        in_specs=[vmem] * 6,
        out_specs=[vmem] * 3,
        scratch_shapes=[block_of(size * tiles)] + [block_of(size * 2)] * 2 + sides,
        input_output_aliases={2: 2},
        compiler_params=large,
        name="rest",
    )(trig, wgt, q, *fringes)
    back = lax.ppermute(send, "span", across)

    def place(other, block, *earlier):
        return pl.pallas_call(
            functools.partial(place_kernel, dims, other),
            out_shape=rows_of(slots * count),
            in_specs=[vmem] + [hbm] * len(earlier),
            out_specs=hbm,
            scratch_shapes=[block_of(count), pltpu.SemaphoreType.DMA((fields,))],
            input_output_aliases={1: 0} if earlier else {},
            compiler_params=pltpu.CompilerParams(vmem_limit_bytes=8 << 20),
            name="place",
        )(block, *earlier)

    return unflat(place(True, back, place(False, mine)), state.shape)


def extended_2(shard, sides, width):
    for axis, dim in sides:
        size, length = (lax.axis_size(axis), shard.shape[dim])
        up = [(i, (i + 1) % size) for i in range(size)]
        down = [(j, i) for i, j in up]
        last = lax.slice_in_dim(shard, length - width, length, axis=dim)
        leading = lax.slice_in_dim(shard, 0, width, axis=dim)
        before = lax.ppermute(last, axis, up)
        after = lax.ppermute(leading, axis, down)
        shard = jnp.concatenate([before, shard, after], axis=dim)
    return shard


def entering(part, axis, combine, identity):
    place = lax.axis_index(axis)
    gathered = jax.tree.map(lambda a: lax.all_gather(a, axis), part)
    state = jax.tree.map(lambda a, e: jnp.zeros_like(a) + jnp.asarray(e, a.dtype), part, identity)

    def one(step, state):
        return combine(
            state, jax.tree.map(lambda a: lax.dynamic_index_in_dim(a, step, 0, False), gathered)
        )

    return lax.fori_loop(0, place, one, state)


def tendency(center, east, west, north, south, upper, lower, weight, cos_yaw, sin_yaw):
    grad_x = (east - west) * 0.5
    grad_y = (north - south) * 0.5
    grad_z = (upper - lower) * 0.5
    laplace = east + west + north + south + upper + lower - 6.0 * center
    vel_u = center[..., 1, :, :, :]
    vel_v = center[..., 2, :, :, :]
    vel_w = center[..., 3, :, :, :]
    dux = grad_x[..., 1, :, :, :]
    dvy = grad_y[..., 2, :, :, :]
    dwz = grad_z[..., 3, :, :, :]
    duy = grad_y[..., 1, :, :, :]
    duz = grad_z[..., 1, :, :, :]
    strain = dux * dux + dvy * dvy + dwz * dwz + duy * duy + duz * duz
    viscous = VISC * jnp.sqrt(1.0 + strain)
    speed = U_MEAN + vel_u
    flow = -(
        jnp.expand_dims(speed, -4) * grad_x
        + jnp.expand_dims(vel_v, -4) * grad_y
        + jnp.expand_dims(vel_w, -4) * grad_z
    )
    flow = flow + jnp.expand_dims(viscous, -4) * laplace
    normal = speed * cos_yaw + vel_v * sin_yaw
    thrust = THRUST * normal * jnp.abs(normal) * weight
    extra = jnp.stack(
        [
            -(dux + dvy + dwz),
            -grad_x[..., 0, :, :, :] - thrust * cos_yaw,
            -grad_y[..., 0, :, :, :] - thrust * sin_yaw,
            -grad_z[..., 0, :, :, :],
        ],
        axis=-4,
    )
    return flow + extra


def extended(fields):
    padded = extended_2(fields, (("span", 2), ("vert", 3)), 1)
    vert_at = lax.axis_index("vert")
    bottom = jnp.where(vert_at == 0, 0.0, padded[:, :, :, :1, :])
    summit = jnp.where(vert_at == lax.axis_size("vert") - 1, 0.0, padded[:, :, :, -1:, :])
    padded = jnp.concatenate([bottom, padded[:, :, :, 1:-1, :], summit], axis=3)
    return padded


def stencil(fields, padded, weight, cos_yaw, sin_yaw):
    east = jnp.roll(fields, -1, axis=4)
    west = jnp.roll(fields, 1, axis=4)
    north = padded[:, :, 2:, 1:-1, :]
    south = padded[:, :, :-2, 1:-1, :]
    upper = padded[:, :, 1:-1, 2:, :]
    lower = padded[:, :, 1:-1, :-2, :]
    return tendency(fields, east, west, north, south, upper, lower, weight, cos_yaw, sin_yaw)


def rate(fields, weight, cos_yaw, sin_yaw):
    return stencil(fields, extended(fields), weight, cos_yaw, sin_yaw)


def make_weight(turbine_x, turbine_y, along_y, along_z, total_y, total_z, active, length):
    along_x = jnp.arange(length, dtype=jnp.int32)
    hit_x = (along_x[None, None, :] == turbine_x[:, :, None]).astype(jnp.float32)
    hit_y = ((along_y[None, None, :] - turbine_y[:, :, None]) % total_y < DISK).astype(jnp.float32)
    plane = jnp.einsum("dky,dkx->dyx", hit_y, hit_x, precision=lax.Precision.HIGHEST)
    lower_half = (along_z < total_z // 2).astype(jnp.float32)
    return plane[:, :, None, :] * lower_half[None, None, :, None] * active[:, None, None, None]


def first_held(earlier, later):
    keep = earlier[1] > 0.0
    return (jnp.where(keep, earlier[0], later[0]), jnp.maximum(earlier[1], later[1]))


def body_general(state, turbine_x, turbine_y, yaw_index):
    slots = state.shape[0]
    rows_y = state.shape[2]
    rows_z = state.shape[3]
    total_y = rows_y * lax.axis_size("span")
    total_z = rows_z * lax.axis_size("vert")
    domain = lax.axis_index("case") * slots + jnp.arange(slots, dtype=jnp.int32)
    active = (domain > 0).astype(jnp.float32)
    along_y = lax.axis_index("span") * rows_y + jnp.arange(rows_y, dtype=jnp.int32)
    along_z = lax.axis_index("vert") * rows_z + jnp.arange(rows_z, dtype=jnp.int32)
    weight = make_weight(turbine_x, turbine_y, along_y, along_z, total_y, total_z, active, state.shape[4])
    angle = (yaw_index.astype(jnp.float32) - 3.5) * YAW_STEP
    cos_yaw = jnp.cos(angle)[:, None, None, None]
    sin_yaw = jnp.sin(angle)[:, None, None, None]
    width = state.shape[4] // 4
    ramp = 0.5 * (1.0 - jnp.cos(jnp.pi * (jnp.arange(width, dtype=jnp.float32) + 1.0) / width))
    case_at = lax.axis_index("case")
    for _ in range(STEPS):
        first = rate(state, weight, cos_yaw, sin_yaw)
        middle = state + TIME_STEP * first
        second = rate(middle, weight, cos_yaw, sin_yaw)
        state = state + 0.5 * TIME_STEP * (first + second)
        front = state[..., :width]
        own_fringe = front[0]
        marker = jnp.ones((), jnp.float32)
        blank = (jnp.zeros_like(own_fringe), jnp.zeros((), jnp.float32))
        passed = entering((own_fringe, marker), "case", first_held, blank)
        source = jnp.where(case_at == 0, own_fringe, passed[0])
        front = front + ramp * (source[None] - front)
        state = jnp.concatenate([front, state[..., width:]], axis=4)
    return state


def body_any(state, turbine_x, turbine_y, yaw_index):
    slots, _, ry, rz, x = state.shape
    fits = lax.axis_size("span") == 2 and slots == 2 and lax.axis_size("vert") % 2 == 0
    fits = fits and ry == 8 and rz % 8 == 0 and x == 4 * LANES
    chosen = body if fits else body_general
    return chosen(state, turbine_x, turbine_y, yaw_index)


def solution(mesh):
    return jax.shard_map(
        body_any,
        mesh=mesh,
        in_specs=(
            P("case", None, "span", "vert", None),
            P("case", None),
            P("case", None),
            P("case"),
        ),
        out_specs=P("case", None, "span", "vert", None),
        check_vma=False,
    )
```

profile of v0, /device:TPU:1, one launch (start us, length us, event | category | flops | bytes accessed | tf_op | source)
XLA Modules:
  0.0 71.8 jit_solution(16480572896002654353)
XLA Ops:
  0.0 1.2 %copy-done = f32[2,4,8,8,512]{4,3,2,1,0:T(8,128)S(1)} copy-done((f32[2,4,8,8,512]{4,3,2,1,0:T(8,128)S(1)}, f32[2,4,8,8,512]{4,3,2,1,0:T(8,128)}, u32[]{:S(2)}) %copy-start) | copy-done | bytes 1048600
  1.4 5.0 %collective-permute-start.7 = (f32[288,128]{1,0:T(8,128)S(1)}, f32[288,128]{1,0:T(8,128)S(1)}, u32[]{:S(2)}, u32[]{:S(2)}) collective-permute-start(f32[288,128]{1,0:T(8,128)S(1)} %fringe.1), channel_id=1, source_target_pairs={{0,16},{1,17},{2,18},{3,19},{4,20},{5,21},{6,22},{7,23}} | collective-permute-start | bytes 442376 | tf_op jit(solution)/shard_map/ppermute | solution.py:408
  6.5 2.5 %collective-permute-done.7 = f32[288,128]{1,0:T(8,128)S(1)} collective-permute-done((f32[288,128]{1,0:T(8,128)S(1)}, f32[288,128]{1,0:T(8,128)S(1)}, u32[]{:S(2)}, u32[]{:S(2)}) %collective-permute-start.7) | collective-permute-done | bytes 147488 | tf_op jit(solution)/shard_map/ppermute | solution.py:408
  9.0 1.3 %collective-permute-start.8 = (f32[288,128]{1,0:T(8,128)S(1)}, f32[288,128]{1,0:T(8,128)S(1)}, u32[]{:S(2)}, u32[]{:S(2)}) collective-permute-start(f32[288,128]{1,0:T(8,128)S(1)} %broadcast_select_fusion), channel_id=1, source_target_pairs={{0,8},{16,24},{1,9},{17,25},{2,10},{18,26},{3,11},{19,27},{4,12},{... | collective-permute-start | bytes 442376 | tf_op jit(solution)/shard_map/ppermute | solution.py:408
  10.3 1.2 %copy-done.1 = f32[2,4,8,8,512]{4,3,2,1,0:T(8,128)S(1)} copy-done((f32[2,4,8,8,512]{4,3,2,1,0:T(8,128)S(1)}, f32[2,4,8,8,512]{4,3,2,1,0:T(8,128)}, u32[]{:S(2)}) %copy-start.1) | copy-done | bytes 1048600
  11.9 1.3 %collective-permute-start = (f32[768,128]{1,0:T(8,128)S(1)}, f32[768,128]{1,0:T(8,128)S(1)}, u32[]{:S(2)}, u32[]{:S(2)}) collective-permute-start(f32[768,128]{1,0:T(8,128)S(1)} %get-tuple-element.16), channel_id=1, source_target_pairs={{0,4},{4,0},{1,5},{5,1},{2,6},{6,2},{3,7},{7,3},{8,12},{12,8},{9,1... | collective-permute-start | bytes 1179656 | tf_op jit(solution)/shard_map/ppermute | solution.py:452
  13.1 0.3 own.1
  13.5 4.8 %collective-permute-start.2 = (f32[768,128]{1,0:T(8,128)S(1)}, f32[768,128]{1,0:T(8,128)S(1)}, u32[]{:S(2)}, u32[]{:S(2)}) collective-permute-start(f32[768,128]{1,0:T(8,128)S(1)} %get-tuple-element.18), channel_id=1, source_target_pairs={{1,2},{2,1},{5,6},{6,5},{9,10},{10,9},{13,14},{14,13},{17,18},{18,... | collective-permute-start | bytes 1179656 | tf_op jit(solution)/shard_map/ppermute | solution.py:462
  18.7 1.2 %collective-permute-start.1 = (f32[256,128]{1,0:T(8,128)S(1)}, f32[256,128]{1,0:T(8,128)S(1)}, u32[]{:S(2)}, u32[]{:S(2)}) collective-permute-start(f32[256,128]{1,0:T(8,128)S(1)} %get-tuple-element.17), channel_id=1, source_target_pairs={{0,4},{4,0},{1,5},{5,1},{2,6},{6,2},{3,7},{7,3},{8,12},{12,8},{9,1... | collective-permute-start | bytes 393224 | tf_op jit(solution)/shard_map/ppermute | solution.py:453
  19.9 7.2 %collective-permute-done.1.got_far = f32[256,128]{1,0:T(8,128)S(1)} collective-permute-done((f32[256,128]{1,0:T(8,128)S(1)}, f32[256,128]{1,0:T(8,128)S(1)}, u32[]{:S(2)}, u32[]{:S(2)}) %collective-permute-start.1) | collective-permute-done | bytes 131104 | tf_op jit(solution)/shard_map/ppermute | solution.py:453
  27.1 2.3 %collective-permute-start.6 = (f32[256,128]{1,0:T(8,128)S(1)}, f32[256,128]{1,0:T(8,128)S(1)}, u32[]{:S(2)}, u32[]{:S(2)}) collective-permute-start(f32[256,128]{1,0:T(8,128)S(1)} %collective-permute-done.1.got_far), channel_id=1, source_target_pairs={{0,1},{1,0},{2,3},{3,2},{4,5},{5,4},{6,7},{7,6},{8,9},{9,8},{10,11... | collective-permute-start | bytes 393224 | tf_op jit(solution)/shard_map/ppermute | solution.py:468
  29.4 3.5 %collective-permute-start.3 = (f32[768,128]{1,0:T(8,128)S(1)}, f32[768,128]{1,0:T(8,128)S(1)}, u32[]{:S(2)}, u32[]{:S(2)}) collective-permute-start(f32[768,128]{1,0:T(8,128)S(1)} %collective-permute-done.got_near), channel_id=1, source_target_pairs={{1,2},{2,1},{5,6},{6,5},{9,10},{10,9},{13,14},{14,13},{17,18},{18,... | collective-permute-start | bytes 1179656 | tf_op jit(solution)/shard_map/ppermute | solution.py:466
  33.1 2.0 %collective-permute-start.10 = (f32[576,128]{1,0:T(8,128)S(1)}, f32[576,128]{1,0:T(8,128)S(1)}, u32[]{:S(2)}, u32[]{:S(2)}) collective-permute-start(f32[576,128]{1,0:T(8,128)S(1)} %pad_maximum_fusion.p_own), channel_id=1, source_target_pairs={{1,2},{2,1},{5,6},{6,5},{9,10},{10,9},{13,14},{14,13},{17,18},{18,... | collective-permute-start | bytes 884744 | tf_op jit(solution)/shard_map/ppermute | solution.py:471
  35.2 0.7 copy-done.2
  35.8 0.7 copy-done.3
  36.5 0.7 copy-done.4
  37.2 0.7 weights.1
  37.9 0.7 collective-permute-done.3.out_got
  38.5 6.5 %first.1.q_in = f32[11264,128]{1,0:T(8,128)S(1)} custom-call(f32[3,8,128]{2,1,0:T(8,128)S(1)} %get-tuple-element.13.trig, f32[2,2,4,2,8,128]{5,4,3,2,1,0:T(8,128)S(1)} %get-tuple-element.14.wgt, f32[1024,128]{1,0:T(8,128)S(1)} %get-tuple-element.15.own, f32[768,128]{1,0:T(8,128)S(1)} %collective-permute-done.got_near, ...), custom_call_target="tpu_custom_call" | custom-call | tf_op jit(solution)/shard_map/first/pallas_call | solution.py:489
  45.1 16.3 %rest.1 = (f32[1024,128]{1,0:T(8,128)S(1)}, f32[1024,128]{1,0:T(8,128)S(1)}, f32[11264,128]{1,0:T(8,128)S(1)}) custom-call(f32[3,8,128]{2,1,0:T(8,128)S(1)} %get-tuple-element.13.trig, f32[2,2,4,2,8,128]{5,4,3,2,1,0:T(8,128)S(1)} %get-tuple-element.14.wgt, f32[11264,128]{1,0:T(8,128)S(1)} %first.1.q_in, ...), custom_call_target="tpu_custom_call", output_to_operand_aliasing={{2}: (2, {})} | custom-call | tf_op jit(solution)/shard_map/rest/pallas_call | solution.py:498
  61.3 1.3 %collective-permute-start.12 = (f32[1024,128]{1,0:T(8,128)S(1)}, f32[1024,128]{1,0:T(8,128)S(1)}, u32[]{:S(2)}, u32[]{:S(2)}) collective-permute-start(f32[1024,128]{1,0:T(8,128)S(1)} %get-tuple-element.19), channel_id=1, source_target_pairs={{0,4},{4,0},{1,5},{5,1},{2,6},{6,2},{3,7},{7,3},{8,12},{12,8},{9,1... | collective-permute-start | bytes 1572872 | tf_op jit(solution)/shard_map/ppermute | solution.py:508
  62.6 0.8 %place.2.refs_1_ = f32[2048,128]{1,0:T(8,128)} custom-call(f32[1024,128]{1,0:T(8,128)S(1)} %get-tuple-element.20.refs_0_), custom_call_target="tpu_custom_call" | custom-call | tf_op jit(solution)/shard_map/place/pallas_call | solution.py:511
  63.5 7.5 %collective-permute-done.12.refs_0_ = f32[1024,128]{1,0:T(8,128)S(1)} collective-permute-done((f32[1024,128]{1,0:T(8,128)S(1)}, f32[1024,128]{1,0:T(8,128)S(1)}, u32[]{:S(2)}, u32[]{:S(2)}) %collective-permute-start.12) | collective-permute-done | bytes 524320 | tf_op jit(solution)/shard_map/ppermute | solution.py:508
  70.9 0.8 %place.3 = f32[2048,128]{1,0:T(8,128)} custom-call(f32[1024,128]{1,0:T(8,128)S(1)} %collective-permute-done.12.refs_0_, f32[2048,128]{1,0:T(8,128)} %place.2.refs_1_), custom_call_target="tpu_custom_call", output_to_operand_aliasing={{}: (1, {})} | custom-call | tf_op jit(solution)/shard_map/place/pallas_call | solution.py:511
  (23 shorter events, 1.0 us)
Async XLA Ops:
  0.0 1.2 %copy-start = (f32[2,4,8,8,512]{4,3,2,1,0:T(8,128)S(1)}, f32[2,4,8,8,512]{4,3,2,1,0:T(8,128)}, u32[]{:S(2)}) copy-start(f32[2,4,8,8,512]{4,3,2,1,0:T(8,128)} %param.4) | copy-start | bytes 3145732
  1.4 7.6 %collective-permute-start.7 = (f32[288,128]{1,0:T(8,128)S(1)}, f32[288,128]{1,0:T(8,128)S(1)}, u32[]{:S(2)}, u32[]{:S(2)}) collective-permute-start(f32[288,128]{1,0:T(8,128)S(1)} %fringe.1), channel_id=1, source_target_pairs={{0,16},{1,17},{2,18},{3,19},{4,20},{5,21},{6,22},{7,23}} | collective-permute-start | bytes 442376 | tf_op jit(solution)/shard_map/ppermute | solution.py:408
  9.0 9.3 %collective-permute-start.8 = (f32[288,128]{1,0:T(8,128)S(1)}, f32[288,128]{1,0:T(8,128)S(1)}, u32[]{:S(2)}, u32[]{:S(2)}) collective-permute-start(f32[288,128]{1,0:T(8,128)S(1)} %broadcast_select_fusion), channel_id=1, source_target_pairs={{0,8},{16,24},{1,9},{17,25},{2,10},{18,26},{3,11},{19,27},{4,12},{... | collective-permute-start | bytes 442376 | tf_op jit(solution)/shard_map/ppermute | solution.py:408
  10.3 1.2 %copy-start.1 = (f32[2,4,8,8,512]{4,3,2,1,0:T(8,128)S(1)}, f32[2,4,8,8,512]{4,3,2,1,0:T(8,128)}, u32[]{:S(2)}) copy-start(f32[2,4,8,8,512]{4,3,2,1,0:T(8,128)} %param.4) | copy-start | bytes 3145732
  11.9 17.6 %collective-permute-start = (f32[768,128]{1,0:T(8,128)S(1)}, f32[768,128]{1,0:T(8,128)S(1)}, u32[]{:S(2)}, u32[]{:S(2)}) collective-permute-start(f32[768,128]{1,0:T(8,128)S(1)} %get-tuple-element.16), channel_id=1, source_target_pairs={{0,4},{4,0},{1,5},{5,1},{2,6},{6,2},{3,7},{7,3},{8,12},{12,8},{9,1... | collective-permute-start | bytes 1179656 | tf_op jit(solution)/shard_map/ppermute | solution.py:452
  13.5 19.6 %collective-permute-start.2 = (f32[768,128]{1,0:T(8,128)S(1)}, f32[768,128]{1,0:T(8,128)S(1)}, u32[]{:S(2)}, u32[]{:S(2)}) collective-permute-start(f32[768,128]{1,0:T(8,128)S(1)} %get-tuple-element.18), channel_id=1, source_target_pairs={{1,2},{2,1},{5,6},{6,5},{9,10},{10,9},{13,14},{14,13},{17,18},{18,... | collective-permute-start | bytes 1179656 | tf_op jit(solution)/shard_map/ppermute | solution.py:462
  18.4 11.1 %collective-permute-start.9 = (f32[288,128]{1,0:T(8,128)S(1)}, f32[288,128]{1,0:T(8,128)S(1)}, u32[]{:S(2)}, u32[]{:S(2)}) collective-permute-start(f32[288,128]{1,0:T(8,128)S(1)} %broadcast_select_fusion.1), channel_id=1, source_target_pairs={{0,4},{4,0},{1,5},{5,1},{2,6},{6,2},{3,7},{7,3},{8,12},{12,8},{9,1... | collective-permute-start | bytes 442376 | tf_op jit(solution)/shard_map/ppermute | solution.py:465
  18.7 8.4 %collective-permute-start.1 = (f32[256,128]{1,0:T(8,128)S(1)}, f32[256,128]{1,0:T(8,128)S(1)}, u32[]{:S(2)}, u32[]{:S(2)}) collective-permute-start(f32[256,128]{1,0:T(8,128)S(1)} %get-tuple-element.17), channel_id=1, source_target_pairs={{0,4},{4,0},{1,5},{5,1},{2,6},{6,2},{3,7},{7,3},{8,12},{12,8},{9,1... | collective-permute-start | bytes 393224 | tf_op jit(solution)/shard_map/ppermute | solution.py:453
  19.9 18.0 %collective-permute-start.4 = (f32[1024,128]{1,0:T(8,128)S(1)}, f32[1024,128]{1,0:T(8,128)S(1)}, u32[]{:S(2)}, u32[]{:S(2)}) collective-permute-start(f32[1024,128]{1,0:T(8,128)S(1)} %get-tuple-element.15.own), channel_id=1, source_target_pairs={{0,1},{1,0},{2,3},{3,2},{4,5},{5,4},{6,7},{7,6},{8,9},{9,8},{10,11... | collective-permute-start | bytes 1572872 | tf_op jit(solution)/shard_map/ppermute | solution.py:463
  27.1 5.9 %collective-permute-start.6 = (f32[256,128]{1,0:T(8,128)S(1)}, f32[256,128]{1,0:T(8,128)S(1)}, u32[]{:S(2)}, u32[]{:S(2)}) collective-permute-start(f32[256,128]{1,0:T(8,128)S(1)} %collective-permute-done.1.got_far), channel_id=1, source_target_pairs={{0,1},{1,0},{2,3},{3,2},{4,5},{5,4},{6,7},{7,6},{8,9},{9,8},{10,11... | collective-permute-start | bytes 393224 | tf_op jit(solution)/shard_map/ppermute | solution.py:468
  29.4 8.4 %collective-permute-start.5 = (f32[768,128]{1,0:T(8,128)S(1)}, f32[768,128]{1,0:T(8,128)S(1)}, u32[]{:S(2)}, u32[]{:S(2)}) collective-permute-start(f32[768,128]{1,0:T(8,128)S(1)} %collective-permute-done.got_near), channel_id=1, source_target_pairs={{0,1},{1,0},{2,3},{3,2},{4,5},{5,4},{6,7},{7,6},{8,9},{9,8},{10,11... | collective-permute-start | bytes 1179656 | tf_op jit(solution)/shard_map/ppermute | solution.py:467
  29.4 9.1 %collective-permute-start.3 = (f32[768,128]{1,0:T(8,128)S(1)}, f32[768,128]{1,0:T(8,128)S(1)}, u32[]{:S(2)}, u32[]{:S(2)}) collective-permute-start(f32[768,128]{1,0:T(8,128)S(1)} %collective-permute-done.got_near), channel_id=1, source_target_pairs={{1,2},{2,1},{5,6},{6,5},{9,10},{10,9},{13,14},{14,13},{17,18},{18,... | collective-permute-start | bytes 1179656 | tf_op jit(solution)/shard_map/ppermute | solution.py:466
  33.0 12.0 %collective-permute-start.11 = (f32[576,128]{1,0:T(8,128)S(1)}, f32[576,128]{1,0:T(8,128)S(1)}, u32[]{:S(2)}, u32[]{:S(2)}) collective-permute-start(f32[576,128]{1,0:T(8,128)S(1)} %pad_maximum_fusion.p_own), channel_id=1, source_target_pairs={{0,1},{1,0},{2,3},{3,2},{4,5},{5,4},{6,7},{7,6},{8,9},{9,8},{10,11... | collective-permute-start | bytes 884744 | tf_op jit(solution)/shard_map/ppermute | solution.py:471
  33.1 11.9 %collective-permute-start.10 = (f32[576,128]{1,0:T(8,128)S(1)}, f32[576,128]{1,0:T(8,128)S(1)}, u32[]{:S(2)}, u32[]{:S(2)}) collective-permute-start(f32[576,128]{1,0:T(8,128)S(1)} %pad_maximum_fusion.p_own), channel_id=1, source_target_pairs={{1,2},{2,1},{5,6},{6,5},{9,10},{10,9},{13,14},{14,13},{17,18},{18,... | collective-permute-start | bytes 884744 | tf_op jit(solution)/shard_map/ppermute | solution.py:471
  35.1 0.7 copy-start.2
  35.8 0.7 copy-start.3
  36.5 0.7 copy-start.4
  61.3 9.6 %collective-permute-start.12 = (f32[1024,128]{1,0:T(8,128)S(1)}, f32[1024,128]{1,0:T(8,128)S(1)}, u32[]{:S(2)}, u32[]{:S(2)}) collective-permute-start(f32[1024,128]{1,0:T(8,128)S(1)} %get-tuple-element.19), channel_id=1, source_target_pairs={{0,4},{4,0},{1,5},{5,1},{2,6},{6,2},{3,7},{7,3},{8,12},{12,8},{9,1... | collective-permute-start | bytes 1572872 | tf_op jit(solution)/shard_map/ppermute | solution.py:508
where the time goes:
time: 72.1 us; the launch traced here: 71.8 us
  Pallas kernels  26 us (36%)
  starting transfers between devices  23.2 us (32%)
  waiting for transfers between devices  17.9 us (25%)
  local copies, waits for them, and re-layouts  4.45 us (6%)
    pallas_call x1, Pallas kernels, body(): pl.pallas_call(functools.partial(rest_kernel, dims), out_shape=[rows_of(c...  16.3 us
    ppermute x1, waiting for transfers between devices, body(): back = lax.ppermute(send, 'span', across)  7.49 us
    ppermute x1, waiting for transfers between devices, body(): got_far = lax.ppermute(away_far, 'span', across)  7.21 us
    pallas_call x1, Pallas kernels, body(): pl.pallas_call(functools.partial(first_kernel, dims), out_shape=rows_of(s...  6.49 us
    ppermute x2, starting transfers between devices, spread(): moved = lax.ppermute(value, axis, pairs)  6.34 us
    ppermute x1, starting transfers between devices, body(): out_own = lax.ppermute(near, 'vert', outer)  4.84 us
    unnamed x10, local copies, waits for them, and re-layouts  4.45 us
    ppermute x1, starting transfers between devices, body(): out_got = lax.ppermute(got_near, 'vert', outer)  3.53 us
  transfers between devices with their start and end apart: 13, of which 4 were waited for; matrix products, arithmetic and copies ran while one was open for 0% of the time, Pallas kernels for 12%

commit v1 on v0

--- a/solution.py
+++ b/solution.py
@@ -141,7 +141,8 @@
         self.lane = lax.broadcasted_iota(jnp.int32, (8, LANES), 1)
         self.first_lane = self.lane == 0
         self.last_lane = self.lane == LANES - 1
-        self.cos_yaw, self.sin_yaw, self.ramp = trig[0], trig[1], trig[2]
+        if trig is not None:
+            self.cos_yaw, self.sin_yaw, self.ramp = trig[0], trig[1], trig[2]
 
     def put(self, dst, width, f, t, z, group, value):
         start = pl.multiple_of(((f * width + t) * self.rows + z + 1) * self.store, 8)
@@ -163,12 +164,13 @@
 
                 pl.when((z < self.dlo) | (z >= self.dhi))(clear)
 
-    def stage(self, src, base, dst, width, k, wgt=None, pq=None, outs=None):
+    def stage(self, src, base, dst, width, k, wgt=None, pq=None, out=None, chosen=None):
         second = k % 2 == 0
         fields, ry, rz, tiles = self.dims
         rows, store, ext, groups, one = self.rows, self.store, self.ext, self.groups, self.one
         dlo, dhi, gate = self.dlo, self.dhi, self.gate
         cos_yaw, sin_yaw, ramp = self.cos_yaw, self.sin_yaw, self.ramp
+        chosen = range(groups) if chosen is None else chosen
         first_lane, last_lane, sides0, sides1 = self.first_lane, self.last_lane, *self.sides
 
         def at(ref, f, t, g, z, dy=0):
@@ -193,7 +195,7 @@
             if wgt is not None:
                 on = jnp.where(z < gate, 1, 0)
             for t in range(width):
-                for g in range(groups):
+                for g in chosen:
                     shift(z + 1, following, t, g)
                     c = [at(src, f, t, g, z) for f in range(fields)]
                     gx, gy, gz, lap = [], [], [], []
@@ -234,8 +236,7 @@
                                 new = new + ramp * (pq[pl.ds(start + (ROW0 + 8 * g), 8), :] - new)
                         else:
                             new = c[f] + rate[f]
-                        if outs is not None:
-                            out = outs[0] if g < groups // 2 else outs[1]
+                        if out is not None:
                             start = ((f * tiles + t) * rz + z - HALO) * ry + 8 * (g % (groups // 2))
                             new = new * (1.0 / SCALES[f])
                             out[pl.ds(pl.multiple_of(start, 8), 8), :] = new
@@ -246,7 +247,7 @@
         count = jnp.minimum(ext - k, dhi) - first
         first = first - jnp.where(dhi < ext, count & 1, 0)
         for t in range(width):
-            for g in range(groups):
+            for g in chosen:
                 shift(first, sides0, t, g)
 
         def pair(i, carry):
@@ -262,48 +263,54 @@
     return jnp.where(f == 0, SCALES[0], SCALES[1])
 
 
+def fill_rows(cells, q, parts):
+    fields, ry, _, tiles = cells.dims
+
+    def one_field(f, carry):
+        for src, held, taken, half, z_dst, count in parts:
+            for t in range(tiles):
+                for k in range(count):
+                    row = pl.multiple_of(((f * tiles + t) * held + taken + k) * ry, 8)
+                    for g in range(ry // 8):
+                        value = scale_of(f) * src[pl.ds(row + 8 * g, 8), :]
+                        cells.put(q, tiles, f, t, z_dst + k, half * (ry // 8) + g, value)
+        return carry
+
+    lax.fori_loop(0, fields, one_field, 0)
+
+
+def fill_kernel(dims, own, got_near, q):
+    cells = Cells(dims, None)
+    rz = dims[2]
+    rest = rz - HALO
+    near = HALO + jnp.where(cells.even, 0, rest)
+    fill_rows(cells, q, ((own, rz, 0, 0, HALO, rz), (got_near, HALO, 0, 1, near, HALO)))
+
+
 def first_kernel(
-    dims, trig, wgt, own, got_near, got_far, out_own, out_got, in_own, in_near, in_far,
-    q, m, sides0, sides1,
+    dims, trig, wgt, q_in, got_far, out_own, out_got, in_own, in_near, in_far, q, m, sides0, sides1
 ):
-    fields, ry, rz, tiles = dims
+    del q_in
+    _, _, rz, tiles = dims
     cells = Cells(dims, trig)
     cells.sides = sides0, sides1
-    put = cells.put
-
-    def fill(parts):
-        def one_field(f, carry):
-            for src, held, taken, half, z_dst, count in parts:
-                for t in range(tiles):
-                    for k in range(count):
-                        row = pl.multiple_of(((f * tiles + t) * held + taken + k) * ry, 8)
-                        for g in range(ry // 8):
-                            value = scale_of(f) * src[pl.ds(row + 8 * g, 8), :]
-                            put(q, tiles, f, t, z_dst + k, half * (ry // 8) + g, value)
-            return carry
-
-        lax.fori_loop(0, fields, one_field, 0)
 
     def pick(a, b):
         return jnp.where(cells.even, a, b)
 
     above = HALO + rz
     rest = rz - HALO
-    fill(
+    fill_rows(
+        cells,
+        q,
         (
-            (own, rz, 0, 0, HALO, rz),
             (in_own, rz, pick(0, rest), 0, pick(above, 0), HALO),
             (out_own, HALO, 0, 0, pick(0, above), HALO),
-        )
-    )
-    fill(
-        (
-            (got_near, HALO, 0, 1, HALO + pick(0, rest), HALO),
             (got_far, rest, 0, 1, HALO + pick(HALO, 0), rest),
             (out_got, HALO, 0, 1, pick(0, above), HALO),
             (in_near, HALO, pick(0, rest), 1, pick(above + rest, 0), HALO - rest),
             (in_far, rest, 0, 1, pick(above, HALO - rest), rest),
-        )
+        ),
     )
     cells.clear_outside((q, tiles), (m, tiles))
     cells.stage(q, None, m, tiles, 1, wgt)
@@ -311,7 +318,7 @@
 
 
 def rest_kernel(
-    dims, trig, wgt, q_in, p_own, p_out, p_in, mine_ref, send_ref, q, m, pq, pm, sides0, sides1
+    dims, trig, wgt, q_in, p_own, p_out, p_in, send_ref, q, m, pq, pm, sides0, sides1
 ):
     del q_in
     fields, ry, rz, tiles = dims
@@ -367,9 +374,18 @@
             low = jnp.maximum(k + 1, cells.dlo)
             lax.fori_loop(low, jnp.minimum(cells.ext - k - 1, cells.dhi), relax, 0)
         else:
-            last = (mine_ref, send_ref) if step == STEPS - 1 else None
             cells.stage(q, None, m, tiles, k, wgt)
-            cells.stage(m, q, q, tiles, k + 1, wgt, pq, last)
+            if step < STEPS - 1:
+                cells.stage(m, q, q, tiles, k + 1, wgt, pq)
+            else:
+                other_half = range(cells.groups // 2, cells.groups)
+                cells.stage(m, q, None, tiles, k + 1, wgt, pq, send_ref, other_half)
+
+
+def last_kernel(dims, trig, wgt, q, m, pq, mine_ref, sides0, sides1):
+    cells = Cells(dims, trig)
+    cells.sides = sides0, sides1
+    cells.stage(m, q, None, dims[3], HALO, wgt, pq, mine_ref, range(cells.groups // 2))
 
 
 def place_kernel(dims, other, *refs):
@@ -487,25 +503,43 @@
         name="weights",
     )(turbine_x, turbine_y, yaw_index)
     q = pl.pallas_call(
+        functools.partial(fill_kernel, dims),
+        out_shape=rows_of(size * tiles),
+        in_specs=[vmem] * 2,
+        out_specs=vmem,
+        compiler_params=small,
+        name="fill",
+    )(own, got_near)
+    q = pl.pallas_call(
         functools.partial(first_kernel, dims),
         out_shape=rows_of(size * tiles),
-        in_specs=[vmem] * 10,
+        in_specs=[vmem] * 9,
         out_specs=vmem,
         scratch_shapes=[block_of(size * tiles)] + sides,
+        input_output_aliases={2: 0},
         compiler_params=large,
         name="first",
-    )(trig, wgt, own, got_near, got_far, out_own, out_got, in_own, in_near, in_far)
-    mine, send, _ = pl.pallas_call(
+    )(trig, wgt, q, got_far, out_own, out_got, in_own, in_near, in_far)
+    send, q, m, pq = pl.pallas_call(
         functools.partial(rest_kernel, dims),
-        out_shape=[rows_of(count)] * 2 + [rows_of(size * tiles)],
+        out_shape=[rows_of(count)] + [rows_of(size * w) for w in (tiles, tiles, 2)],
         in_specs=[vmem] * 6,
-        out_specs=[vmem] * 3,
-        scratch_shapes=[block_of(size * tiles)] + [block_of(size * 2)] * 2 + sides,
-        input_output_aliases={2: 2},
+        out_specs=[vmem] * 4,
+        scratch_shapes=[block_of(size * 2)] + sides,
+        input_output_aliases={2: 1},
         compiler_params=large,
         name="rest",
     )(trig, wgt, q, *fringes)
     back = lax.ppermute(send, "span", across)
+    mine = pl.pallas_call(
+        functools.partial(last_kernel, dims),
+        out_shape=rows_of(count),
+        in_specs=[vmem] * 5,
+        out_specs=vmem,
+        scratch_shapes=sides,
+        compiler_params=large,
+        name="last",
+    )(trig, wgt, q, m, pq)
 
     def place(other, block, *earlier):
         return pl.pallas_call(

time: 72.1 us -> 71.6 us (level)
  waiting for transfers between devices: 17.9 us -> 17 us
    pallas_call x0 -> x2, Pallas kernels: none -> 1.04 us  [the longest x1 0.88 us: body(): pl.pallas_call(functools.partial(last_kernel, dims), out_shape=rows_of(co...]
    ppermute x1, waiting for transfers between devices: 7.49 us -> 6.74 us  [body(): back = lax.ppermute(send, 'span', across)]
  transfers between devices with their start and end apart: 13 -> 13, of which waited for: 4 -> 4; matrix products, arithmetic and copies ran while one was open for 0% -> 0% of each run, Pallas kernels for 12% -> 13%
where the time goes in v1:
time: 71.6 us; the launch traced here: 71.3 us
  Pallas kernels  26.4 us (37%)
  starting transfers between devices  23.2 us (32%)
  waiting for transfers between devices  17 us (24%)
  local copies, waits for them, and re-layouts  4.45 us (6%)
    pallas_call x1, Pallas kernels, body(): pl.pallas_call(functools.partial(rest_kernel, dims), out_shape=[rows_of(c...  15.7 us
    ppermute x1, waiting for transfers between devices, body(): got_far = lax.ppermute(away_far, 'span', across)  7.21 us
    ppermute x1, waiting for transfers between devices, body(): back = lax.ppermute(send, 'span', across)  6.74 us
    pallas_call x1, Pallas kernels, body(): pl.pallas_call(functools.partial(first_kernel, dims), out_shape=rows_of(s...  6.36 us
    ppermute x2, starting transfers between devices, spread(): moved = lax.ppermute(value, axis, pairs)  6.34 us
    ppermute x1, starting transfers between devices, body(): out_own = lax.ppermute(near, 'vert', outer)  4.84 us
    unnamed x10, local copies, waits for them, and re-layouts  4.45 us
    ppermute x1, starting transfers between devices, body(): out_got = lax.ppermute(got_near, 'vert', outer)  3.53 us
  transfers between devices with their start and end apart: 13, of which 4 were waited for; matrix products, arithmetic and copies ran while one was open for 0% of the time, Pallas kernels for 13%

profile of v1, /device:TPU:1, one launch (start us, length us, event | category | flops | bytes accessed | tf_op | source)
XLA Modules:
  0.0 71.3 jit_solution(11218606076752792683)
XLA Ops:
  0.0 1.2 %copy-done = f32[2,4,8,8,512]{4,3,2,1,0:T(8,128)S(1)} copy-done((f32[2,4,8,8,512]{4,3,2,1,0:T(8,128)S(1)}, f32[2,4,8,8,512]{4,3,2,1,0:T(8,128)}, u32[]{:S(2)}) %copy-start) | copy-done | bytes 1048600
  1.4 5.0 %collective-permute-start.7 = (f32[288,128]{1,0:T(8,128)S(1)}, f32[288,128]{1,0:T(8,128)S(1)}, u32[]{:S(2)}, u32[]{:S(2)}) collective-permute-start(f32[288,128]{1,0:T(8,128)S(1)} %fringe.1), channel_id=1, source_target_pairs={{0,16},{1,17},{2,18},{3,19},{4,20},{5,21},{6,22},{7,23}} | collective-permute-start | bytes 442376 | tf_op jit(solution)/shard_map/ppermute | solution.py:424
  6.5 2.5 %collective-permute-done.7 = f32[288,128]{1,0:T(8,128)S(1)} collective-permute-done((f32[288,128]{1,0:T(8,128)S(1)}, f32[288,128]{1,0:T(8,128)S(1)}, u32[]{:S(2)}, u32[]{:S(2)}) %collective-permute-start.7) | collective-permute-done | bytes 147488 | tf_op jit(solution)/shard_map/ppermute | solution.py:424
  9.0 1.3 %collective-permute-start.8 = (f32[288,128]{1,0:T(8,128)S(1)}, f32[288,128]{1,0:T(8,128)S(1)}, u32[]{:S(2)}, u32[]{:S(2)}) collective-permute-start(f32[288,128]{1,0:T(8,128)S(1)} %broadcast_select_fusion), channel_id=1, source_target_pairs={{0,8},{16,24},{1,9},{17,25},{2,10},{18,26},{3,11},{19,27},{4,12},{... | collective-permute-start | bytes 442376 | tf_op jit(solution)/shard_map/ppermute | solution.py:424
  10.3 1.2 %copy-done.1 = f32[2,4,8,8,512]{4,3,2,1,0:T(8,128)S(1)} copy-done((f32[2,4,8,8,512]{4,3,2,1,0:T(8,128)S(1)}, f32[2,4,8,8,512]{4,3,2,1,0:T(8,128)}, u32[]{:S(2)}) %copy-start.1) | copy-done | bytes 1048600
  11.9 1.3 %collective-permute-start = (f32[768,128]{1,0:T(8,128)S(1)}, f32[768,128]{1,0:T(8,128)S(1)}, u32[]{:S(2)}, u32[]{:S(2)}) collective-permute-start(f32[768,128]{1,0:T(8,128)S(1)} %get-tuple-element.18), channel_id=1, source_target_pairs={{0,4},{4,0},{1,5},{5,1},{2,6},{6,2},{3,7},{7,3},{8,12},{12,8},{9,1... | collective-permute-start | bytes 1179656 | tf_op jit(solution)/shard_map/ppermute | solution.py:468
  13.5 4.8 %collective-permute-start.2 = (f32[768,128]{1,0:T(8,128)S(1)}, f32[768,128]{1,0:T(8,128)S(1)}, u32[]{:S(2)}, u32[]{:S(2)}) collective-permute-start(f32[768,128]{1,0:T(8,128)S(1)} %get-tuple-element.20), channel_id=1, source_target_pairs={{1,2},{2,1},{5,6},{6,5},{9,10},{10,9},{13,14},{14,13},{17,18},{18,... | collective-permute-start | bytes 1179656 | tf_op jit(solution)/shard_map/ppermute | solution.py:478
  18.7 1.2 %collective-permute-start.1 = (f32[256,128]{1,0:T(8,128)S(1)}, f32[256,128]{1,0:T(8,128)S(1)}, u32[]{:S(2)}, u32[]{:S(2)}) collective-permute-start(f32[256,128]{1,0:T(8,128)S(1)} %get-tuple-element.19), channel_id=1, source_target_pairs={{0,4},{4,0},{1,5},{5,1},{2,6},{6,2},{3,7},{7,3},{8,12},{12,8},{9,1... | collective-permute-start | bytes 393224 | tf_op jit(solution)/shard_map/ppermute | solution.py:469
  19.9 7.2 %collective-permute-done.1.got_far = f32[256,128]{1,0:T(8,128)S(1)} collective-permute-done((f32[256,128]{1,0:T(8,128)S(1)}, f32[256,128]{1,0:T(8,128)S(1)}, u32[]{:S(2)}, u32[]{:S(2)}) %collective-permute-start.1) | collective-permute-done | bytes 131104 | tf_op jit(solution)/shard_map/ppermute | solution.py:469
  27.1 2.3 %collective-permute-start.6 = (f32[256,128]{1,0:T(8,128)S(1)}, f32[256,128]{1,0:T(8,128)S(1)}, u32[]{:S(2)}, u32[]{:S(2)}) collective-permute-start(f32[256,128]{1,0:T(8,128)S(1)} %collective-permute-done.1.got_far), channel_id=1, source_target_pairs={{0,1},{1,0},{2,3},{3,2},{4,5},{5,4},{6,7},{7,6},{8,9},{9,8},{10,11... | collective-permute-start | bytes 393224 | tf_op jit(solution)/shard_map/ppermute | solution.py:484
  29.4 3.5 %collective-permute-start.3 = (f32[768,128]{1,0:T(8,128)S(1)}, f32[768,128]{1,0:T(8,128)S(1)}, u32[]{:S(2)}, u32[]{:S(2)}) collective-permute-start(f32[768,128]{1,0:T(8,128)S(1)} %collective-permute-done.got_near), channel_id=1, source_target_pairs={{1,2},{2,1},{5,6},{6,5},{9,10},{10,9},{13,14},{14,13},{17,18},{18,... | collective-permute-start | bytes 1179656 | tf_op jit(solution)/shard_map/ppermute | solution.py:482
  33.1 2.0 %collective-permute-start.10 = (f32[576,128]{1,0:T(8,128)S(1)}, f32[576,128]{1,0:T(8,128)S(1)}, u32[]{:S(2)}, u32[]{:S(2)}) collective-permute-start(f32[576,128]{1,0:T(8,128)S(1)} %pad_maximum_fusion.p_own), channel_id=1, source_target_pairs={{1,2},{2,1},{5,6},{6,5},{9,10},{10,9},{13,14},{14,13},{17,18},{18,... | collective-permute-start | bytes 884744 | tf_op jit(solution)/shard_map/ppermute | solution.py:487
  35.2 0.7 copy-done.2
  35.8 0.7 copy-done.3
  36.5 0.7 copy-done.4
  37.2 0.7 weights.1
  38.0 0.5 collective-permute-done.3.out_got
  38.5 6.4 %first.1.q_in = f32[11264,128]{1,0:T(8,128)S(1)} custom-call(f32[3,8,128]{2,1,0:T(8,128)S(1)} %get-tuple-element.15.trig, f32[2,2,4,2,8,128]{5,4,3,2,1,0:T(8,128)S(1)} %get-tuple-element.16.wgt, f32[11264,128]{1,0:T(8,128)S(1)} %fill.1.q_in, f32[256,128]{1,0:T(8,128)S(1)} %collective-permute-done.1.got_far, ...), custom_call_target="tpu_custom_call", output_to_operand_aliasing={{}: (2, {})} | custom-call | tf_op jit(solution)/shard_map/first/pallas_call | solution.py:513
  44.9 15.7 %rest.1 = (f32[1024,128]{1,0:T(8,128)S(1)}, f32[11264,128]{1,0:T(8,128)S(1)}, f32[11264,128]{1,0:T(8,128)S(1)}, f32[5632,128]{1,0:T(8,128)S(1)}) custom-call(f32[3,8,128]{2,1,0:T(8,128)S(1)} %get-tuple-element.15.trig, f32[2,2,4,2,8,128]{5,4,3,2,1,0:T(8,128)S(1)} %get-tuple-element.16.wgt, ...), custom_call_target="tpu_custom_call", output_to_operand_aliasing={{1}: (2, {})} | custom-call | tf_op jit(solution)/shard_map/rest/pallas_call | solution.py:523
  60.7 1.3 %collective-permute-start.12 = (f32[1024,128]{1,0:T(8,128)S(1)}, f32[1024,128]{1,0:T(8,128)S(1)}, u32[]{:S(2)}, u32[]{:S(2)}) collective-permute-start(f32[1024,128]{1,0:T(8,128)S(1)} %get-tuple-element.21), channel_id=1, source_target_pairs={{0,4},{4,0},{1,5},{5,1},{2,6},{6,2},{3,7},{7,3},{8,12},{12,8},{9,1... | collective-permute-start | bytes 1572872 | tf_op jit(solution)/shard_map/ppermute | solution.py:533
  61.9 0.9 %last.1.refs_0_ = f32[1024,128]{1,0:T(8,128)S(1)} custom-call(f32[3,8,128]{2,1,0:T(8,128)S(1)} %get-tuple-element.15.trig, f32[2,2,4,2,8,128]{5,4,3,2,1,0:T(8,128)S(1)} %get-tuple-element.16.wgt, f32[11264,128]{1,0:T(8,128)S(1)} %get-tuple-element.22.q, f32[11264,128]{1,0:T(8,128)S(1)} %get-tuple-element.23.m, f32[5632,128]{1,0:T(8,128)S(1)} %get-tuple-element.24.pq), custom_call_target="tpu_custom_call" | custom-call | tf_op jit(solution)/shard_map/last/pallas_call | solution.py:534
  62.8 0.8 %place.2.refs_1_ = f32[2048,128]{1,0:T(8,128)} custom-call(f32[1024,128]{1,0:T(8,128)S(1)} %last.1.refs_0_), custom_call_target="tpu_custom_call" | custom-call | tf_op jit(solution)/shard_map/place/pallas_call | solution.py:545
  63.7 6.7 %collective-permute-done.12.refs_0_ = f32[1024,128]{1,0:T(8,128)S(1)} collective-permute-done((f32[1024,128]{1,0:T(8,128)S(1)}, f32[1024,128]{1,0:T(8,128)S(1)}, u32[]{:S(2)}, u32[]{:S(2)}) %collective-permute-start.12) | collective-permute-done | bytes 524320 | tf_op jit(solution)/shard_map/ppermute | solution.py:533
  70.4 0.8 %place.3 = f32[2048,128]{1,0:T(8,128)} custom-call(f32[1024,128]{1,0:T(8,128)S(1)} %collective-permute-done.12.refs_0_, f32[2048,128]{1,0:T(8,128)} %place.2.refs_1_), custom_call_target="tpu_custom_call", output_to_operand_aliasing={{}: (1, {})} | custom-call | tf_op jit(solution)/shard_map/place/pallas_call | solution.py:545
  (25 shorter events, 1.5 us)
Async XLA Ops:
  0.0 1.2 %copy-start = (f32[2,4,8,8,512]{4,3,2,1,0:T(8,128)S(1)}, f32[2,4,8,8,512]{4,3,2,1,0:T(8,128)}, u32[]{:S(2)}) copy-start(f32[2,4,8,8,512]{4,3,2,1,0:T(8,128)} %param.4) | copy-start | bytes 3145732
  1.4 7.6 %collective-permute-start.7 = (f32[288,128]{1,0:T(8,128)S(1)}, f32[288,128]{1,0:T(8,128)S(1)}, u32[]{:S(2)}, u32[]{:S(2)}) collective-permute-start(f32[288,128]{1,0:T(8,128)S(1)} %fringe.1), channel_id=1, source_target_pairs={{0,16},{1,17},{2,18},{3,19},{4,20},{5,21},{6,22},{7,23}} | collective-permute-start | bytes 442376 | tf_op jit(solution)/shard_map/ppermute | solution.py:424
  9.0 9.3 %collective-permute-start.8 = (f32[288,128]{1,0:T(8,128)S(1)}, f32[288,128]{1,0:T(8,128)S(1)}, u32[]{:S(2)}, u32[]{:S(2)}) collective-permute-start(f32[288,128]{1,0:T(8,128)S(1)} %broadcast_select_fusion), channel_id=1, source_target_pairs={{0,8},{16,24},{1,9},{17,25},{2,10},{18,26},{3,11},{19,27},{4,12},{... | collective-permute-start | bytes 442376 | tf_op jit(solution)/shard_map/ppermute | solution.py:424
  10.3 1.2 %copy-start.1 = (f32[2,4,8,8,512]{4,3,2,1,0:T(8,128)S(1)}, f32[2,4,8,8,512]{4,3,2,1,0:T(8,128)}, u32[]{:S(2)}) copy-start(f32[2,4,8,8,512]{4,3,2,1,0:T(8,128)} %param.4) | copy-start | bytes 3145732
  11.9 17.6 %collective-permute-start = (f32[768,128]{1,0:T(8,128)S(1)}, f32[768,128]{1,0:T(8,128)S(1)}, u32[]{:S(2)}, u32[]{:S(2)}) collective-permute-start(f32[768,128]{1,0:T(8,128)S(1)} %get-tuple-element.18), channel_id=1, source_target_pairs={{0,4},{4,0},{1,5},{5,1},{2,6},{6,2},{3,7},{7,3},{8,12},{12,8},{9,1... | collective-permute-start | bytes 1179656 | tf_op jit(solution)/shard_map/ppermute | solution.py:468
  13.5 19.6 %collective-permute-start.2 = (f32[768,128]{1,0:T(8,128)S(1)}, f32[768,128]{1,0:T(8,128)S(1)}, u32[]{:S(2)}, u32[]{:S(2)}) collective-permute-start(f32[768,128]{1,0:T(8,128)S(1)} %get-tuple-element.20), channel_id=1, source_target_pairs={{1,2},{2,1},{5,6},{6,5},{9,10},{10,9},{13,14},{14,13},{17,18},{18,... | collective-permute-start | bytes 1179656 | tf_op jit(solution)/shard_map/ppermute | solution.py:478
  18.4 11.1 %collective-permute-start.9 = (f32[288,128]{1,0:T(8,128)S(1)}, f32[288,128]{1,0:T(8,128)S(1)}, u32[]{:S(2)}, u32[]{:S(2)}) collective-permute-start(f32[288,128]{1,0:T(8,128)S(1)} %broadcast_select_fusion.1), channel_id=1, source_target_pairs={{0,4},{4,0},{1,5},{5,1},{2,6},{6,2},{3,7},{7,3},{8,12},{12,8},{9,1... | collective-permute-start | bytes 442376 | tf_op jit(solution)/shard_map/ppermute | solution.py:481
  18.7 8.4 %collective-permute-start.1 = (f32[256,128]{1,0:T(8,128)S(1)}, f32[256,128]{1,0:T(8,128)S(1)}, u32[]{:S(2)}, u32[]{:S(2)}) collective-permute-start(f32[256,128]{1,0:T(8,128)S(1)} %get-tuple-element.19), channel_id=1, source_target_pairs={{0,4},{4,0},{1,5},{5,1},{2,6},{6,2},{3,7},{7,3},{8,12},{12,8},{9,1... | collective-permute-start | bytes 393224 | tf_op jit(solution)/shard_map/ppermute | solution.py:469
  19.9 18.1 %collective-permute-start.4 = (f32[1024,128]{1,0:T(8,128)S(1)}, f32[1024,128]{1,0:T(8,128)S(1)}, u32[]{:S(2)}, u32[]{:S(2)}) collective-permute-start(f32[1024,128]{1,0:T(8,128)S(1)} %get-tuple-element.17.own), channel_id=1, source_target_pairs={{0,1},{1,0},{2,3},{3,2},{4,5},{5,4},{6,7},{7,6},{8,9},{9,8},{10,11... | collective-permute-start | bytes 1572872 | tf_op jit(solution)/shard_map/ppermute | solution.py:479
  27.1 5.9 %collective-permute-start.6 = (f32[256,128]{1,0:T(8,128)S(1)}, f32[256,128]{1,0:T(8,128)S(1)}, u32[]{:S(2)}, u32[]{:S(2)}) collective-permute-start(f32[256,128]{1,0:T(8,128)S(1)} %collective-permute-done.1.got_far), channel_id=1, source_target_pairs={{0,1},{1,0},{2,3},{3,2},{4,5},{5,4},{6,7},{7,6},{8,9},{9,8},{10,11... | collective-permute-start | bytes 393224 | tf_op jit(solution)/shard_map/ppermute | solution.py:484
  29.4 8.6 %collective-permute-start.5 = (f32[768,128]{1,0:T(8,128)S(1)}, f32[768,128]{1,0:T(8,128)S(1)}, u32[]{:S(2)}, u32[]{:S(2)}) collective-permute-start(f32[768,128]{1,0:T(8,128)S(1)} %collective-permute-done.got_near), channel_id=1, source_target_pairs={{0,1},{1,0},{2,3},{3,2},{4,5},{5,4},{6,7},{7,6},{8,9},{9,8},{10,11... | collective-permute-start | bytes 1179656 | tf_op jit(solution)/shard_map/ppermute | solution.py:483
  29.4 9.1 %collective-permute-start.3 = (f32[768,128]{1,0:T(8,128)S(1)}, f32[768,128]{1,0:T(8,128)S(1)}, u32[]{:S(2)}, u32[]{:S(2)}) collective-permute-start(f32[768,128]{1,0:T(8,128)S(1)} %collective-permute-done.got_near), channel_id=1, source_target_pairs={{1,2},{2,1},{5,6},{6,5},{9,10},{10,9},{13,14},{14,13},{17,18},{18,... | collective-permute-start | bytes 1179656 | tf_op jit(solution)/shard_map/ppermute | solution.py:482
  33.0 11.9 %collective-permute-start.11 = (f32[576,128]{1,0:T(8,128)S(1)}, f32[576,128]{1,0:T(8,128)S(1)}, u32[]{:S(2)}, u32[]{:S(2)}) collective-permute-start(f32[576,128]{1,0:T(8,128)S(1)} %pad_maximum_fusion.p_own), channel_id=1, source_target_pairs={{0,1},{1,0},{2,3},{3,2},{4,5},{5,4},{6,7},{7,6},{8,9},{9,8},{10,11... | collective-permute-start | bytes 884744 | tf_op jit(solution)/shard_map/ppermute | solution.py:487
  33.1 11.8 %collective-permute-start.10 = (f32[576,128]{1,0:T(8,128)S(1)}, f32[576,128]{1,0:T(8,128)S(1)}, u32[]{:S(2)}, u32[]{:S(2)}) collective-permute-start(f32[576,128]{1,0:T(8,128)S(1)} %pad_maximum_fusion.p_own), channel_id=1, source_target_pairs={{1,2},{2,1},{5,6},{6,5},{9,10},{10,9},{13,14},{14,13},{17,18},{18,... | collective-permute-start | bytes 884744 | tf_op jit(solution)/shard_map/ppermute | solution.py:487
  35.1 0.7 copy-start.2
  35.8 0.7 copy-start.3
  36.5 0.7 copy-start.4
  60.7 9.8 %collective-permute-start.12 = (f32[1024,128]{1,0:T(8,128)S(1)}, f32[1024,128]{1,0:T(8,128)S(1)}, u32[]{:S(2)}, u32[]{:S(2)}) collective-permute-start(f32[1024,128]{1,0:T(8,128)S(1)} %get-tuple-element.21), channel_id=1, source_target_pairs={{0,4},{4,0},{1,5},{5,1},{2,6},{6,2},{3,7},{7,3},{8,12},{12,8},{9,1... | collective-permute-start | bytes 1572872 | tf_op jit(solution)/shard_map/ppermute | solution.py:533

commit v2 on v1

--- a/solution.py
+++ b/solution.py
@@ -164,9 +164,9 @@
 
                 pl.when((z < self.dlo) | (z >= self.dhi))(clear)
 
-    def stage(self, src, base, dst, width, k, wgt=None, pq=None, out=None, chosen=None):
+    def stage(self, src, base, dst, width, k, wgt=None, pq=None, out=None, chosen=None, lo=0, hi=None, held=None):
         second = k % 2 == 0
-        fields, ry, rz, tiles = self.dims
+        fields, ry, _, tiles = self.dims
         rows, store, ext, groups, one = self.rows, self.store, self.ext, self.groups, self.one
         dlo, dhi, gate = self.dlo, self.dhi, self.gate
         cos_yaw, sin_yaw, ramp = self.cos_yaw, self.sin_yaw, self.ramp
@@ -237,14 +237,15 @@
                         else:
                             new = c[f] + rate[f]
                         if out is not None:
-                            start = ((f * tiles + t) * rz + z - HALO) * ry + 8 * (g % (groups // 2))
+                            start = (f * tiles + t) * held[1] + z - HALO - held[0]
+                            start = start * ry + 8 * (g % (groups // 2))
                             new = new * (1.0 / SCALES[f])
                             out[pl.ds(pl.multiple_of(start, 8), 8), :] = new
                         else:
                             self.put(dst, width, f, t, z, g, new)
 
-        first = jnp.maximum(k, dlo)
-        count = jnp.minimum(ext - k, dhi) - first
+        first = jnp.maximum(max(k, lo), dlo)
+        count = jnp.minimum(min(ext - k, ext if hi is None else hi), dhi) - first
         first = first - jnp.where(dhi < ext, count & 1, 0)
         for t in range(width):
             for g in chosen:
@@ -287,10 +288,20 @@
     fill_rows(cells, q, ((own, rz, 0, 0, HALO, rz), (got_near, HALO, 0, 1, near, HALO)))
 
 
+def early_kernel(dims, trig, wgt, q_in, got_far, q, m, sides0, sides1):
+    del q_in
+    rz, tiles = dims[2:]
+    rest = rz - HALO
+    cells = Cells(dims, trig)
+    cells.sides = sides0, sides1
+    fill_rows(cells, q, ((got_far, rest, 0, 1, HALO + jnp.where(cells.even, HALO, 0), rest),))
+    cells.stage(q, None, m, tiles, 1, wgt, lo=HALO + 1, hi=HALO + rz - 1)
+
+
 def first_kernel(
-    dims, trig, wgt, q_in, got_far, out_own, out_got, in_own, in_near, in_far, q, m, sides0, sides1
+    dims, trig, wgt, q_in, m_in, out_own, out_got, in_own, in_near, in_far, q, m, sides0, sides1
 ):
-    del q_in
+    del q_in, m_in
     _, _, rz, tiles = dims
     cells = Cells(dims, trig)
     cells.sides = sides0, sides1
@@ -306,14 +317,14 @@
         (
             (in_own, rz, pick(0, rest), 0, pick(above, 0), HALO),
             (out_own, HALO, 0, 0, pick(0, above), HALO),
-            (got_far, rest, 0, 1, HALO + pick(HALO, 0), rest),
             (out_got, HALO, 0, 1, pick(0, above), HALO),
             (in_near, HALO, pick(0, rest), 1, pick(above + rest, 0), HALO - rest),
             (in_far, rest, 0, 1, pick(above, HALO - rest), rest),
         ),
     )
     cells.clear_outside((q, tiles), (m, tiles))
-    cells.stage(q, None, m, tiles, 1, wgt)
+    cells.stage(q, None, m, tiles, 1, wgt, hi=HALO + 1)
+    cells.stage(q, None, m, tiles, 1, wgt, lo=HALO + rz - 1)
     cells.stage(m, q, q, tiles, 2, wgt)
 
 
@@ -374,32 +385,51 @@
             low = jnp.maximum(k + 1, cells.dlo)
             lax.fori_loop(low, jnp.minimum(cells.ext - k - 1, cells.dhi), relax, 0)
         else:
-            cells.stage(q, None, m, tiles, k, wgt)
             if step < STEPS - 1:
+                cells.stage(q, None, m, tiles, k, wgt)
                 cells.stage(m, q, q, tiles, k + 1, wgt, pq)
             else:
+                middle = HALO + rz // 2
                 other_half = range(cells.groups // 2, cells.groups)
-                cells.stage(m, q, None, tiles, k + 1, wgt, pq, send_ref, other_half)
+                cells.stage(q, None, m, tiles, k, wgt, hi=middle + 1)
+                lower = dict(hi=middle, held=(0, rz // 2))
+                cells.stage(m, q, None, tiles, k + 1, wgt, pq, send_ref, other_half, **lower)
+
+
+def upper_kernel(dims, trig, wgt, q, m_in, pq, send_ref, m, sides0, sides1):
+    del m_in
+    rz, tiles = dims[2:]
+    cells = Cells(dims, trig)
+    cells.sides = sides0, sides1
+    middle = HALO + rz // 2
+    other_half = range(cells.groups // 2, cells.groups)
+    cells.stage(q, None, m, tiles, HALO - 1, wgt, lo=middle + 1)
+    upper = dict(lo=middle, held=(rz // 2, rz // 2))
+    cells.stage(m, q, None, tiles, HALO, wgt, pq, send_ref, other_half, **upper)
 
 
 def last_kernel(dims, trig, wgt, q, m, pq, mine_ref, sides0, sides1):
     cells = Cells(dims, trig)
     cells.sides = sides0, sides1
-    cells.stage(m, q, None, dims[3], HALO, wgt, pq, mine_ref, range(cells.groups // 2))
-
-
-def place_kernel(dims, other, *refs):
+    own_half = range(cells.groups // 2)
+    cells.stage(m, q, None, dims[3], HALO, wgt, pq, mine_ref, own_half, held=(0, dims[2]))
+
+
+def place_kernel(dims, other, parts, *refs):
     fields, ry, rz, tiles = dims
-    src, out_ref, block, sems = refs[0], refs[-3], refs[-2], refs[-1]
+    out_ref, block, sems = refs[-3:]
     size = ry * tiles * rz
+    count = rz // parts
     slot = lax.axis_index("span")
     slot = 1 - slot if other else slot
     copies = []
     for f in range(fields):
         for y in range(ry):
             for t in range(tiles):
-                value = src[pl.ds((f * tiles + t) * rz * ry + y, rz, stride=ry), :]
-                block[pl.ds(((f * ry + y) * tiles + t) * rz, rz), :] = value
+                for i in range(parts):
+                    source = (f * tiles + t) * count * ry + y
+                    value = refs[i][pl.ds(source, count, stride=ry), :]
+                    block[pl.ds(((f * ry + y) * tiles + t) * rz + i * count, count), :] = value
         start = pl.multiple_of((slot * fields + f) * size, 8)
         part = block.at[pl.ds(f * size, size)]
         copies.append(pltpu.make_async_copy(part, out_ref.at[pl.ds(start, size)], sems.at[f]))
@@ -510,19 +540,30 @@
         compiler_params=small,
         name="fill",
     )(own, got_near)
-    q = pl.pallas_call(
-        functools.partial(first_kernel, dims),
-        out_shape=rows_of(size * tiles),
-        in_specs=[vmem] * 9,
-        out_specs=vmem,
-        scratch_shapes=[block_of(size * tiles)] + sides,
+    q, m = pl.pallas_call(
+        functools.partial(early_kernel, dims),
+        out_shape=[rows_of(size * tiles)] * 2,
+        in_specs=[vmem] * 4,
+        out_specs=[vmem] * 2,
+        scratch_shapes=sides,
         input_output_aliases={2: 0},
         compiler_params=large,
+        name="early",
+    )(trig, wgt, q, got_far)
+    q, m = pl.pallas_call(
+        functools.partial(first_kernel, dims),
+        out_shape=[rows_of(size * tiles)] * 2,
+        in_specs=[vmem] * 9,
+        out_specs=[vmem] * 2,
+        scratch_shapes=sides,
+        input_output_aliases={2: 0, 3: 1},
+        compiler_params=large,
         name="first",
-    )(trig, wgt, q, got_far, out_own, out_got, in_own, in_near, in_far)
-    send, q, m, pq = pl.pallas_call(
+    )(trig, wgt, q, m, out_own, out_got, in_own, in_near, in_far)
+    half_rows = rows_of(count // 2)
+    send_low, q, m, pq = pl.pallas_call(
         functools.partial(rest_kernel, dims),
-        out_shape=[rows_of(count)] + [rows_of(size * w) for w in (tiles, tiles, 2)],
+        out_shape=[half_rows] + [rows_of(size * w) for w in (tiles, tiles, 2)],
         in_specs=[vmem] * 6,
         out_specs=[vmem] * 4,
         scratch_shapes=[block_of(size * 2)] + sides,
@@ -530,7 +571,18 @@
         compiler_params=large,
         name="rest",
     )(trig, wgt, q, *fringes)
-    back = lax.ppermute(send, "span", across)
+    back_low = lax.ppermute(send_low, "span", across)
+    send_high, m = pl.pallas_call(
+        functools.partial(upper_kernel, dims),
+        out_shape=[half_rows, rows_of(size * tiles)],
+        in_specs=[vmem] * 5,
+        out_specs=[vmem] * 2,
+        scratch_shapes=sides,
+        input_output_aliases={3: 1},
+        compiler_params=large,
+        name="upper",
+    )(trig, wgt, q, m, pq)
+    back_high = lax.ppermute(send_high, "span", across)
     mine = pl.pallas_call(
         functools.partial(last_kernel, dims),
         out_shape=rows_of(count),
@@ -541,19 +593,20 @@
         name="last",
     )(trig, wgt, q, m, pq)
 
-    def place(other, block, *earlier):
+    def place(other, blocks, *earlier):
+        parts = len(blocks)
         return pl.pallas_call(
-            functools.partial(place_kernel, dims, other),
+            functools.partial(place_kernel, dims, other, parts),
             out_shape=rows_of(slots * count),
-            in_specs=[vmem] + [hbm] * len(earlier),
+            in_specs=[vmem] * parts + [hbm] * len(earlier),
             out_specs=hbm,
             scratch_shapes=[block_of(count), pltpu.SemaphoreType.DMA((fields,))],
-            input_output_aliases={1: 0} if earlier else {},
-            compiler_params=pltpu.CompilerParams(vmem_limit_bytes=8 << 20),
+            input_output_aliases={parts: 0} if earlier else {},
+            compiler_params=small,
             name="place",
-        )(block, *earlier)
-
-    return unflat(place(True, back, place(False, mine)), state.shape)
+        )(*blocks, *earlier)
+
+    return unflat(place(True, (back_low, back_high), place(False, (mine,))), state.shape)
 
 
 def extended_2(shard, sides, width):

time: 71.6 us -> 72.3 us (level)
    pallas_call x4 -> x6, Pallas kernels: 23.8 us -> 24.3 us  [the longest x1 14.7 us: body(): pl.pallas_call(functools.partial(rest_kernel, dims), out_shape=[half_rows...]
    ppermute x1 -> x2, starting transfers between devices: 1.28 us -> 1.6 us  [the longest x1 1.28 us: body(): back_low = lax.ppermute(send_low, 'span', across)]
    ppermute x1 -> x2, waiting for transfers between devices: 6.74 us -> 6.95 us  [the longest x1 3.74 us: body(): back_low = lax.ppermute(send_low, 'span', across)]
  transfers between devices with their start and end apart: 13 -> 14, of which waited for: 4 -> 4; matrix products, arithmetic and copies ran while one was open for 0% -> 0% of each run, Pallas kernels for 13% -> 16%
where the time goes in v2:
time: 72.3 us; the launch traced here: 72 us
  Pallas kernels  26.9 us (37%)
  starting transfers between devices  23.6 us (33%)
  waiting for transfers between devices  16.7 us (23%)
  local copies, waits for them, and re-layouts  4.45 us (6%)
    pallas_call x1, Pallas kernels, body(): pl.pallas_call(functools.partial(rest_kernel, dims), out_shape=[half_rows...  14.7 us
    ppermute x1, waiting for transfers between devices, body(): got_far = lax.ppermute(away_far, 'span', across)  7.21 us
    ppermute x2, starting transfers between devices, spread(): moved = lax.ppermute(value, axis, pairs)  6.34 us
    pallas_call x1, Pallas kernels, body(): pl.pallas_call(functools.partial(first_kernel, dims), out_shape=[rows_of(...  5.49 us
    ppermute x1, starting transfers between devices, body(): out_own = lax.ppermute(near, 'vert', outer)  4.84 us
    unnamed x10, local copies, waits for them, and re-layouts  4.45 us
    ppermute x1, waiting for transfers between devices, body(): back_low = lax.ppermute(send_low, 'span', across)  3.74 us
    ppermute x1, waiting for transfers between devices, body(): back_high = lax.ppermute(send_high, 'span', across)  3.21 us
  transfers between devices with their start and end apart: 14, of which 4 were waited for; matrix products, arithmetic and copies ran while one was open for 0% of the time, Pallas kernels for 16%

profile of v2, /device:TPU:1, one launch (start us, length us, event | category | flops | bytes accessed | tf_op | source)
XLA Modules:
  0.0 72.0 jit_solution(10980000372240823070)
XLA Ops:
  0.0 1.2 %copy-done = f32[2,4,8,8,512]{4,3,2,1,0:T(8,128)S(1)} copy-done((f32[2,4,8,8,512]{4,3,2,1,0:T(8,128)S(1)}, f32[2,4,8,8,512]{4,3,2,1,0:T(8,128)}, u32[]{:S(2)}) %copy-start) | copy-done | bytes 1048600
  1.4 5.0 %collective-permute-start.7 = (f32[288,128]{1,0:T(8,128)S(1)}, f32[288,128]{1,0:T(8,128)S(1)}, u32[]{:S(2)}, u32[]{:S(2)}) collective-permute-start(f32[288,128]{1,0:T(8,128)S(1)} %fringe.1), channel_id=1, source_target_pairs={{0,16},{1,17},{2,18},{3,19},{4,20},{5,21},{6,22},{7,23}} | collective-permute-start | bytes 442376 | tf_op jit(solution)/shard_map/ppermute | solution.py:454
  6.5 2.5 %collective-permute-done.7 = f32[288,128]{1,0:T(8,128)S(1)} collective-permute-done((f32[288,128]{1,0:T(8,128)S(1)}, f32[288,128]{1,0:T(8,128)S(1)}, u32[]{:S(2)}, u32[]{:S(2)}) %collective-permute-start.7) | collective-permute-done | bytes 147488 | tf_op jit(solution)/shard_map/ppermute | solution.py:454
  9.0 1.3 %collective-permute-start.8 = (f32[288,128]{1,0:T(8,128)S(1)}, f32[288,128]{1,0:T(8,128)S(1)}, u32[]{:S(2)}, u32[]{:S(2)}) collective-permute-start(f32[288,128]{1,0:T(8,128)S(1)} %broadcast_select_fusion), channel_id=1, source_target_pairs={{0,8},{16,24},{1,9},{17,25},{2,10},{18,26},{3,11},{19,27},{4,12},{... | collective-permute-start | bytes 442376 | tf_op jit(solution)/shard_map/ppermute | solution.py:454
  10.3 1.2 %copy-done.1 = f32[2,4,8,8,512]{4,3,2,1,0:T(8,128)S(1)} copy-done((f32[2,4,8,8,512]{4,3,2,1,0:T(8,128)S(1)}, f32[2,4,8,8,512]{4,3,2,1,0:T(8,128)}, u32[]{:S(2)}) %copy-start.1) | copy-done | bytes 1048600
  11.9 1.3 %collective-permute-start = (f32[768,128]{1,0:T(8,128)S(1)}, f32[768,128]{1,0:T(8,128)S(1)}, u32[]{:S(2)}, u32[]{:S(2)}) collective-permute-start(f32[768,128]{1,0:T(8,128)S(1)} %get-tuple-element.23), channel_id=1, source_target_pairs={{0,4},{4,0},{1,5},{5,1},{2,6},{6,2},{3,7},{7,3},{8,12},{12,8},{9,1... | collective-permute-start | bytes 1179656 | tf_op jit(solution)/shard_map/ppermute | solution.py:498
  13.5 4.8 %collective-permute-start.2 = (f32[768,128]{1,0:T(8,128)S(1)}, f32[768,128]{1,0:T(8,128)S(1)}, u32[]{:S(2)}, u32[]{:S(2)}) collective-permute-start(f32[768,128]{1,0:T(8,128)S(1)} %get-tuple-element.27), channel_id=1, source_target_pairs={{1,2},{2,1},{5,6},{6,5},{9,10},{10,9},{13,14},{14,13},{17,18},{18,... | collective-permute-start | bytes 1179656 | tf_op jit(solution)/shard_map/ppermute | solution.py:508
  18.7 1.2 %collective-permute-start.1 = (f32[256,128]{1,0:T(8,128)S(1)}, f32[256,128]{1,0:T(8,128)S(1)}, u32[]{:S(2)}, u32[]{:S(2)}) collective-permute-start(f32[256,128]{1,0:T(8,128)S(1)} %get-tuple-element.24), channel_id=1, source_target_pairs={{0,4},{4,0},{1,5},{5,1},{2,6},{6,2},{3,7},{7,3},{8,12},{12,8},{9,1... | collective-permute-start | bytes 393224 | tf_op jit(solution)/shard_map/ppermute | solution.py:499
  19.9 7.2 %collective-permute-done.1.got_far = f32[256,128]{1,0:T(8,128)S(1)} collective-permute-done((f32[256,128]{1,0:T(8,128)S(1)}, f32[256,128]{1,0:T(8,128)S(1)}, u32[]{:S(2)}, u32[]{:S(2)}) %collective-permute-start.1) | collective-permute-done | bytes 131104 | tf_op jit(solution)/shard_map/ppermute | solution.py:499
  27.1 2.3 %collective-permute-start.6 = (f32[256,128]{1,0:T(8,128)S(1)}, f32[256,128]{1,0:T(8,128)S(1)}, u32[]{:S(2)}, u32[]{:S(2)}) collective-permute-start(f32[256,128]{1,0:T(8,128)S(1)} %collective-permute-done.1.got_far), channel_id=1, source_target_pairs={{0,1},{1,0},{2,3},{3,2},{4,5},{5,4},{6,7},{7,6},{8,9},{9,8},{10,11... | collective-permute-start | bytes 393224 | tf_op jit(solution)/shard_map/ppermute | solution.py:514
  29.4 3.0 %collective-permute-start.3 = (f32[768,128]{1,0:T(8,128)S(1)}, f32[768,128]{1,0:T(8,128)S(1)}, u32[]{:S(2)}, u32[]{:S(2)}) collective-permute-start(f32[768,128]{1,0:T(8,128)S(1)} %collective-permute-done.got_near), channel_id=1, source_target_pairs={{1,2},{2,1},{5,6},{6,5},{9,10},{10,9},{13,14},{14,13},{17,18},{18,... | collective-permute-start | bytes 1179656 | tf_op jit(solution)/shard_map/ppermute | solution.py:512
  32.6 2.5 %collective-permute-start.10 = (f32[576,128]{1,0:T(8,128)S(1)}, f32[576,128]{1,0:T(8,128)S(1)}, u32[]{:S(2)}, u32[]{:S(2)}) collective-permute-start(f32[576,128]{1,0:T(8,128)S(1)} %pad_maximum_fusion.p_own), channel_id=1, source_target_pairs={{1,2},{2,1},{5,6},{6,5},{9,10},{10,9},{13,14},{14,13},{17,18},{18,... | collective-permute-start | bytes 884744 | tf_op jit(solution)/shard_map/ppermute | solution.py:517
  35.9 0.7 copy-done.3
  37.2 0.7 weights.1
  38.1 1.2 %early.1 = (f32[11264,128]{1,0:T(8,128)S(1)}, f32[11264,128]{1,0:T(8,128)S(1)}) custom-call(f32[3,8,128]{2,1,0:T(8,128)S(1)} %get-tuple-element.20.trig, f32[2,2,4,2,8,128]{5,4,3,2,1,0:T(8,128)S(1)} %get-tuple-element.21.wgt, f32[11264,128]{1,0:T(8,128)S(1)} %fill.1.q_in, f32[256,128]{1,0:T(8,128)S(1)} %collective-permute-done.1.got_far), custom_call_target="tpu_custom_call", output_to_operand_aliasing={{0}: (2, {})} | custom-call | tf_op jit(solution)/shard_map/early/pallas_call | solution.py:543
  39.3 5.5 %first.1 = (f32[11264,128]{1,0:T(8,128)S(1)}, f32[11264,128]{1,0:T(8,128)S(1)}) custom-call(f32[3,8,128]{2,1,0:T(8,128)S(1)} %get-tuple-element.20.trig, f32[2,2,4,2,8,128]{5,4,3,2,1,0:T(8,128)S(1)} %get-tuple-element.21.wgt, f32[11264,128]{1,0:T(8,128)S(1)} %get-tuple-element.25.q_in, ...), custom_call_target="tpu_custom_call", output_to_operand_aliasing={{0}: (2, {}), {1}: (3, {})} | custom-call | tf_op jit(solution)/shard_map/first/pallas_call | solution.py:553
  44.8 14.7 %rest.1 = (f32[512,128]{1,0:T(8,128)S(1)}, f32[11264,128]{1,0:T(8,128)S(1)}, f32[11264,128]{1,0:T(8,128)S(1)}, f32[5632,128]{1,0:T(8,128)S(1)}) custom-call(f32[3,8,128]{2,1,0:T(8,128)S(1)} %get-tuple-element.20.trig, f32[2,2,4,2,8,128]{5,4,3,2,1,0:T(8,128)S(1)} %get-tuple-element.21.wgt, ...), custom_call_target="tpu_custom_call", output_to_operand_aliasing={{1}: (2, {})} | custom-call | tf_op jit(solution)/shard_map/rest/pallas_call | solution.py:564
  59.5 1.3 %collective-permute-start.12 = (f32[512,128]{1,0:T(8,128)S(1)}, f32[512,128]{1,0:T(8,128)S(1)}, u32[]{:S(2)}, u32[]{:S(2)}) collective-permute-start(f32[512,128]{1,0:T(8,128)S(1)} %get-tuple-element.29), channel_id=1, source_target_pairs={{0,4},{4,0},{1,5},{5,1},{2,6},{6,2},{3,7},{7,3},{8,12},{12,8},{9,1... | collective-permute-start | bytes 786440 | tf_op jit(solution)/shard_map/ppermute | solution.py:574
  60.8 1.3 %upper.1 = (f32[512,128]{1,0:T(8,128)S(1)}, f32[11264,128]{1,0:T(8,128)S(1)}) custom-call(f32[3,8,128]{2,1,0:T(8,128)S(1)} %get-tuple-element.20.trig, f32[2,2,4,2,8,128]{5,4,3,2,1,0:T(8,128)S(1)} %get-tuple-element.21.wgt, f32[11264,128]{1,0:T(8,128)S(1)} %get-tuple-element.30.q, ...), custom_call_target="tpu_custom_call", output_to_operand_aliasing={{1}: (3, {})} | custom-call | tf_op jit(solution)/shard_map/upper/pallas_call | solution.py:575
  62.4 0.9 %last.1.refs_0_ = f32[1024,128]{1,0:T(8,128)S(1)} custom-call(f32[3,8,128]{2,1,0:T(8,128)S(1)} %get-tuple-element.20.trig, f32[2,2,4,2,8,128]{5,4,3,2,1,0:T(8,128)S(1)} %get-tuple-element.21.wgt, f32[11264,128]{1,0:T(8,128)S(1)} %get-tuple-element.30.q, f32[11264,128]{1,0:T(8,128)S(1)} %get-tuple-element.34.m, f32[5632,128]{1,0:T(8,128)S(1)} %get-tuple-element.32.pq), custom_call_target="tpu_custom_call" | custom-call | tf_op jit(solution)/shard_map/last/pallas_call | solution.py:586
  63.3 0.8 %place.2.refs_2_ = f32[2048,128]{1,0:T(8,128)} custom-call(f32[1024,128]{1,0:T(8,128)S(1)} %last.1.refs_0_), custom_call_target="tpu_custom_call" | custom-call | tf_op jit(solution)/shard_map/place/pallas_call | solution.py:598
  64.1 3.7 %collective-permute-done.12.refs_0_ = f32[512,128]{1,0:T(8,128)S(1)} collective-permute-done((f32[512,128]{1,0:T(8,128)S(1)}, f32[512,128]{1,0:T(8,128)S(1)}, u32[]{:S(2)}, u32[]{:S(2)}) %collective-permute-start.12) | collective-permute-done | bytes 262176 | tf_op jit(solution)/shard_map/ppermute | solution.py:574
  67.9 3.2 %collective-permute-done.13.refs_1_ = f32[512,128]{1,0:T(8,128)S(1)} collective-permute-done((f32[512,128]{1,0:T(8,128)S(1)}, f32[512,128]{1,0:T(8,128)S(1)}, u32[]{:S(2)}, u32[]{:S(2)}) %collective-permute-start.13) | collective-permute-done | bytes 262176 | tf_op jit(solution)/shard_map/ppermute | solution.py:585
  71.1 0.9 %place.3 = f32[2048,128]{1,0:T(8,128)} custom-call(f32[512,128]{1,0:T(8,128)S(1)} %collective-permute-done.12.refs_0_, f32[512,128]{1,0:T(8,128)S(1)} %collective-permute-done.13.refs_1_, f32[2048,128]{1,0:T(8,128)} %place.2.refs_2_), custom_call_target="tpu_custom_call", output_to_operand_aliasing={{}: (2, {})} | custom-call | tf_op jit(solution)/shard_map/place/pallas_call | solution.py:598
  (29 shorter events, 3.2 us)
Async XLA Ops:
  0.0 1.2 %copy-start = (f32[2,4,8,8,512]{4,3,2,1,0:T(8,128)S(1)}, f32[2,4,8,8,512]{4,3,2,1,0:T(8,128)}, u32[]{:S(2)}) copy-start(f32[2,4,8,8,512]{4,3,2,1,0:T(8,128)} %param.4) | copy-start | bytes 3145732
  1.4 7.6 %collective-permute-start.7 = (f32[288,128]{1,0:T(8,128)S(1)}, f32[288,128]{1,0:T(8,128)S(1)}, u32[]{:S(2)}, u32[]{:S(2)}) collective-permute-start(f32[288,128]{1,0:T(8,128)S(1)} %fringe.1), channel_id=1, source_target_pairs={{0,16},{1,17},{2,18},{3,19},{4,20},{5,21},{6,22},{7,23}} | collective-permute-start | bytes 442376 | tf_op jit(solution)/shard_map/ppermute | solution.py:454
  9.0 9.3 %collective-permute-start.8 = (f32[288,128]{1,0:T(8,128)S(1)}, f32[288,128]{1,0:T(8,128)S(1)}, u32[]{:S(2)}, u32[]{:S(2)}) collective-permute-start(f32[288,128]{1,0:T(8,128)S(1)} %broadcast_select_fusion), channel_id=1, source_target_pairs={{0,8},{16,24},{1,9},{17,25},{2,10},{18,26},{3,11},{19,27},{4,12},{... | collective-permute-start | bytes 442376 | tf_op jit(solution)/shard_map/ppermute | solution.py:454
  10.3 1.2 %copy-start.1 = (f32[2,4,8,8,512]{4,3,2,1,0:T(8,128)S(1)}, f32[2,4,8,8,512]{4,3,2,1,0:T(8,128)}, u32[]{:S(2)}) copy-start(f32[2,4,8,8,512]{4,3,2,1,0:T(8,128)} %param.4) | copy-start | bytes 3145732
  11.9 17.6 %collective-permute-start = (f32[768,128]{1,0:T(8,128)S(1)}, f32[768,128]{1,0:T(8,128)S(1)}, u32[]{:S(2)}, u32[]{:S(2)}) collective-permute-start(f32[768,128]{1,0:T(8,128)S(1)} %get-tuple-element.23), channel_id=1, source_target_pairs={{0,4},{4,0},{1,5},{5,1},{2,6},{6,2},{3,7},{7,3},{8,12},{12,8},{9,1... | collective-permute-start | bytes 1179656 | tf_op jit(solution)/shard_map/ppermute | solution.py:498
  13.5 21.7 %collective-permute-start.2 = (f32[768,128]{1,0:T(8,128)S(1)}, f32[768,128]{1,0:T(8,128)S(1)}, u32[]{:S(2)}, u32[]{:S(2)}) collective-permute-start(f32[768,128]{1,0:T(8,128)S(1)} %get-tuple-element.27), channel_id=1, source_target_pairs={{1,2},{2,1},{5,6},{6,5},{9,10},{10,9},{13,14},{14,13},{17,18},{18,... | collective-permute-start | bytes 1179656 | tf_op jit(solution)/shard_map/ppermute | solution.py:508
  18.4 14.1 %collective-permute-start.9 = (f32[288,128]{1,0:T(8,128)S(1)}, f32[288,128]{1,0:T(8,128)S(1)}, u32[]{:S(2)}, u32[]{:S(2)}) collective-permute-start(f32[288,128]{1,0:T(8,128)S(1)} %broadcast_select_fusion.1), channel_id=1, source_target_pairs={{0,4},{4,0},{1,5},{5,1},{2,6},{6,2},{3,7},{7,3},{8,12},{12,8},{9,1... | collective-permute-start | bytes 442376 | tf_op jit(solution)/shard_map/ppermute | solution.py:511
  18.7 8.4 %collective-permute-start.1 = (f32[256,128]{1,0:T(8,128)S(1)}, f32[256,128]{1,0:T(8,128)S(1)}, u32[]{:S(2)}, u32[]{:S(2)}) collective-permute-start(f32[256,128]{1,0:T(8,128)S(1)} %get-tuple-element.24), channel_id=1, source_target_pairs={{0,4},{4,0},{1,5},{5,1},{2,6},{6,2},{3,7},{7,3},{8,12},{12,8},{9,1... | collective-permute-start | bytes 393224 | tf_op jit(solution)/shard_map/ppermute | solution.py:499
  19.9 19.4 %collective-permute-start.4 = (f32[1024,128]{1,0:T(8,128)S(1)}, f32[1024,128]{1,0:T(8,128)S(1)}, u32[]{:S(2)}, u32[]{:S(2)}) collective-permute-start(f32[1024,128]{1,0:T(8,128)S(1)} %get-tuple-element.22.own), channel_id=1, source_target_pairs={{0,1},{1,0},{2,3},{3,2},{4,5},{5,4},{6,7},{7,6},{8,9},{9,8},{10,11... | collective-permute-start | bytes 1572872 | tf_op jit(solution)/shard_map/ppermute | solution.py:509
  27.1 5.5 %collective-permute-start.6 = (f32[256,128]{1,0:T(8,128)S(1)}, f32[256,128]{1,0:T(8,128)S(1)}, u32[]{:S(2)}, u32[]{:S(2)}) collective-permute-start(f32[256,128]{1,0:T(8,128)S(1)} %collective-permute-done.1.got_far), channel_id=1, source_target_pairs={{0,1},{1,0},{2,3},{3,2},{4,5},{5,4},{6,7},{7,6},{8,9},{9,8},{10,11... | collective-permute-start | bytes 393224 | tf_op jit(solution)/shard_map/ppermute | solution.py:514
  29.4 9.9 %collective-permute-start.3 = (f32[768,128]{1,0:T(8,128)S(1)}, f32[768,128]{1,0:T(8,128)S(1)}, u32[]{:S(2)}, u32[]{:S(2)}) collective-permute-start(f32[768,128]{1,0:T(8,128)S(1)} %collective-permute-done.got_near), channel_id=1, source_target_pairs={{1,2},{2,1},{5,6},{6,5},{9,10},{10,9},{13,14},{14,13},{17,18},{18,... | collective-permute-start | bytes 1179656 | tf_op jit(solution)/shard_map/ppermute | solution.py:512
  32.5 6.8 %collective-permute-start.5 = (f32[768,128]{1,0:T(8,128)S(1)}, f32[768,128]{1,0:T(8,128)S(1)}, u32[]{:S(2)}, u32[]{:S(2)}) collective-permute-start(f32[768,128]{1,0:T(8,128)S(1)} %collective-permute-done.got_near), channel_id=1, source_target_pairs={{0,1},{1,0},{2,3},{3,2},{4,5},{5,4},{6,7},{7,6},{8,9},{9,8},{10,11... | collective-permute-start | bytes 1179656 | tf_op jit(solution)/shard_map/ppermute | solution.py:513
  32.6 12.2 %collective-permute-start.10 = (f32[576,128]{1,0:T(8,128)S(1)}, f32[576,128]{1,0:T(8,128)S(1)}, u32[]{:S(2)}, u32[]{:S(2)}) collective-permute-start(f32[576,128]{1,0:T(8,128)S(1)} %pad_maximum_fusion.p_own), channel_id=1, source_target_pairs={{1,2},{2,1},{5,6},{6,5},{9,10},{10,9},{13,14},{14,13},{17,18},{18,... | collective-permute-start | bytes 884744 | tf_op jit(solution)/shard_map/ppermute | solution.py:517
  35.1 9.7 %collective-permute-start.11 = (f32[576,128]{1,0:T(8,128)S(1)}, f32[576,128]{1,0:T(8,128)S(1)}, u32[]{:S(2)}, u32[]{:S(2)}) collective-permute-start(f32[576,128]{1,0:T(8,128)S(1)} %pad_maximum_fusion.p_own), channel_id=1, source_target_pairs={{0,1},{1,0},{2,3},{3,2},{4,5},{5,4},{6,7},{7,6},{8,9},{9,8},{10,11... | collective-permute-start | bytes 884744 | tf_op jit(solution)/shard_map/ppermute | solution.py:517
  35.2 0.7 copy-start.2
  35.9 0.7 copy-start.3
  36.6 0.7 copy-start.4
  59.5 8.4 %collective-permute-start.12 = (f32[512,128]{1,0:T(8,128)S(1)}, f32[512,128]{1,0:T(8,128)S(1)}, u32[]{:S(2)}, u32[]{:S(2)}) collective-permute-start(f32[512,128]{1,0:T(8,128)S(1)} %get-tuple-element.29), channel_id=1, source_target_pairs={{0,4},{4,0},{1,5},{5,1},{2,6},{6,2},{3,7},{7,3},{8,12},{12,8},{9,1... | collective-permute-start | bytes 786440 | tf_op jit(solution)/shard_map/ppermute | solution.py:574
  62.1 9.0 %collective-permute-start.13 = (f32[512,128]{1,0:T(8,128)S(1)}, f32[512,128]{1,0:T(8,128)S(1)}, u32[]{:S(2)}, u32[]{:S(2)}) collective-permute-start(f32[512,128]{1,0:T(8,128)S(1)} %get-tuple-element.33), channel_id=1, source_target_pairs={{0,4},{4,0},{1,5},{5,1},{2,6},{6,2},{3,7},{7,3},{8,12},{12,8},{9,1... | collective-permute-start | bytes 786440 | tf_op jit(solution)/shard_map/ppermute | solution.py:585

commit v3 on v2

--- a/solution.py
+++ b/solution.py
@@ -244,8 +244,8 @@
                         else:
                             self.put(dst, width, f, t, z, g, new)
 
-        first = jnp.maximum(max(k, lo), dlo)
-        count = jnp.minimum(min(ext - k, ext if hi is None else hi), dhi) - first
+        first = jnp.maximum(jnp.maximum(k, lo), dlo)
+        count = jnp.minimum(jnp.minimum(ext - k, ext if hi is None else hi), dhi) - first
         first = first - jnp.where(dhi < ext, count & 1, 0)
         for t in range(width):
             for g in chosen:
@@ -288,21 +288,11 @@
     fill_rows(cells, q, ((own, rz, 0, 0, HALO, rz), (got_near, HALO, 0, 1, near, HALO)))
 
 
-def early_kernel(dims, trig, wgt, q_in, got_far, q, m, sides0, sides1):
+def early_kernel(
+    dims, trig, wgt, q_in, got_far, in_own, in_near, in_far, q, m, sides0, sides1
+):
     del q_in
     rz, tiles = dims[2:]
-    rest = rz - HALO
-    cells = Cells(dims, trig)
-    cells.sides = sides0, sides1
-    fill_rows(cells, q, ((got_far, rest, 0, 1, HALO + jnp.where(cells.even, HALO, 0), rest),))
-    cells.stage(q, None, m, tiles, 1, wgt, lo=HALO + 1, hi=HALO + rz - 1)
-
-
-def first_kernel(
-    dims, trig, wgt, q_in, m_in, out_own, out_got, in_own, in_near, in_far, q, m, sides0, sides1
-):
-    del q_in, m_in
-    _, _, rz, tiles = dims
     cells = Cells(dims, trig)
     cells.sides = sides0, sides1
 
@@ -315,16 +305,31 @@
         cells,
         q,
         (
+            (got_far, rest, 0, 1, HALO + pick(HALO, 0), rest),
             (in_own, rz, pick(0, rest), 0, pick(above, 0), HALO),
-            (out_own, HALO, 0, 0, pick(0, above), HALO),
-            (out_got, HALO, 0, 1, pick(0, above), HALO),
             (in_near, HALO, pick(0, rest), 1, pick(above + rest, 0), HALO - rest),
             (in_far, rest, 0, 1, pick(above, HALO - rest), rest),
         ),
     )
+    last = HALO + above - 1
+    cells.stage(q, None, m, tiles, 1, wgt, lo=pick(HALO + 1, 1), hi=pick(last, above - 1))
+
+
+def first_kernel(dims, trig, wgt, q_in, m_in, out_own, out_got, q, m, sides0, sides1):
+    del q_in, m_in
+    rz, tiles = dims[2:]
+    cells = Cells(dims, trig)
+    cells.sides = sides0, sides1
+
+    def pick(a, b):
+        return jnp.where(cells.even, a, b)
+
+    above = HALO + rz
+    side = pick(0, above)
+    fill_rows(cells, q, ((out_own, HALO, 0, 0, side, HALO), (out_got, HALO, 0, 1, side, HALO)))
     cells.clear_outside((q, tiles), (m, tiles))
-    cells.stage(q, None, m, tiles, 1, wgt, hi=HALO + 1)
-    cells.stage(q, None, m, tiles, 1, wgt, lo=HALO + rz - 1)
+    last = HALO + above - 1
+    cells.stage(q, None, m, tiles, 1, wgt, lo=pick(1, above - 1), hi=pick(HALO + 1, last))
     cells.stage(m, q, q, tiles, 2, wgt)
 
 
@@ -543,23 +548,23 @@
     q, m = pl.pallas_call(
         functools.partial(early_kernel, dims),
         out_shape=[rows_of(size * tiles)] * 2,
-        in_specs=[vmem] * 4,
+        in_specs=[vmem] * 7,
         out_specs=[vmem] * 2,
         scratch_shapes=sides,
         input_output_aliases={2: 0},
         compiler_params=large,
         name="early",
-    )(trig, wgt, q, got_far)
+    )(trig, wgt, q, got_far, in_own, in_near, in_far)
     q, m = pl.pallas_call(
         functools.partial(first_kernel, dims),
         out_shape=[rows_of(size * tiles)] * 2,
-        in_specs=[vmem] * 9,
+        in_specs=[vmem] * 6,
         out_specs=[vmem] * 2,
         scratch_shapes=sides,
         input_output_aliases={2: 0, 3: 1},
         compiler_params=large,
         name="first",
-    )(trig, wgt, q, m, out_own, out_got, in_own, in_near, in_far)
+    )(trig, wgt, q, m, out_own, out_got)
     half_rows = rows_of(count // 2)
     send_low, q, m, pq = pl.pallas_call(
         functools.partial(rest_kernel, dims),

time: 72.3 us -> 77.1 us (1.066)
  waiting for transfers between devices: 16.7 us -> 23.3 us
  starting transfers between devices: 23.6 us -> 22 us
    ppermute x1, waiting for transfers between devices: 7.21 us -> 13.8 us  [body(): got_far = lax.ppermute(away_far, 'span', across)]
    ppermute x1, starting transfers between devices: 4.84 us -> 3.02 us  [body(): out_own = lax.ppermute(near, 'vert', outer)]
    ppermute x1, starting transfers between devices: 0.01 us -> 1.59 us  [body(): in_own = lax.ppermute(own, 'vert', inner)]
    ppermute x1, starting transfers between devices: 2.31 us -> 0.89 us  [body(): in_far = lax.ppermute(got_far, 'vert', inner)]
    pallas_call x1, Pallas kernels: 5.49 us -> 4.21 us  [body(): pl.pallas_call(functools.partial(first_kernel, dims), out_shape=[rows_of(...]
    pallas_call x1, Pallas kernels: 1.19 us -> 2.31 us  [body(): pl.pallas_call(functools.partial(early_kernel, dims), out_shape=[rows_of(...]
  transfers between devices with their start and end apart: 14 -> 14, of which waited for: 4 -> 4; matrix products, arithmetic and copies ran while one was open for 0% -> 0% of each run, Pallas kernels for 16% -> 14%
where the time goes in v3:
time: 77.1 us; the launch traced here: 76.8 us
  Pallas kernels  26.8 us (35%)
  waiting for transfers between devices  23.3 us (30%)
  starting transfers between devices  22 us (29%)
  local copies, waits for them, and re-layouts  4.45 us (6%)
    pallas_call x1, Pallas kernels, body(): pl.pallas_call(functools.partial(rest_kernel, dims), out_shape=[half_rows...  14.7 us
    ppermute x1, waiting for transfers between devices, body(): got_far = lax.ppermute(away_far, 'span', across)  13.8 us
    ppermute x2, starting transfers between devices, spread(): moved = lax.ppermute(value, axis, pairs)  6.34 us
    unnamed x10, local copies, waits for them, and re-layouts  4.45 us
    pallas_call x1, Pallas kernels, body(): pl.pallas_call(functools.partial(first_kernel, dims), out_shape=[rows_of(...  4.21 us
    ppermute x1, waiting for transfers between devices, body(): back_low = lax.ppermute(send_low, 'span', across)  3.74 us
    ppermute x1, waiting for transfers between devices, body(): back_high = lax.ppermute(send_high, 'span', across)  3.2 us
    ppermute x2, starting transfers between devices, body(): fringes.append(lax.ppermute(fringes[0], 'vert', pairs))  3.11 us
  transfers between devices with their start and end apart: 14, of which 4 were waited for; matrix products, arithmetic and copies ran while one was open for 0% of the time, Pallas kernels for 14%

profile of v3, /device:TPU:1, one launch (start us, length us, event | category | flops | bytes accessed | tf_op | source)
XLA Modules:
  0.0 76.8 jit_solution(8701098448166790782)
XLA Ops:
  0.0 1.2 %copy-done = f32[2,4,8,8,512]{4,3,2,1,0:T(8,128)S(1)} copy-done((f32[2,4,8,8,512]{4,3,2,1,0:T(8,128)S(1)}, f32[2,4,8,8,512]{4,3,2,1,0:T(8,128)}, u32[]{:S(2)}) %copy-start) | copy-done | bytes 1048600
  1.4 5.0 %collective-permute-start.7 = (f32[288,128]{1,0:T(8,128)S(1)}, f32[288,128]{1,0:T(8,128)S(1)}, u32[]{:S(2)}, u32[]{:S(2)}) collective-permute-start(f32[288,128]{1,0:T(8,128)S(1)} %fringe.1), channel_id=1, source_target_pairs={{0,16},{1,17},{2,18},{3,19},{4,20},{5,21},{6,22},{7,23}} | collective-permute-start | bytes 442376 | tf_op jit(solution)/shard_map/ppermute | solution.py:459
  6.5 2.5 %collective-permute-done.7 = f32[288,128]{1,0:T(8,128)S(1)} collective-permute-done((f32[288,128]{1,0:T(8,128)S(1)}, f32[288,128]{1,0:T(8,128)S(1)}, u32[]{:S(2)}, u32[]{:S(2)}) %collective-permute-start.7) | collective-permute-done | bytes 147488 | tf_op jit(solution)/shard_map/ppermute | solution.py:459
  9.0 1.3 %collective-permute-start.8 = (f32[288,128]{1,0:T(8,128)S(1)}, f32[288,128]{1,0:T(8,128)S(1)}, u32[]{:S(2)}, u32[]{:S(2)}) collective-permute-start(f32[288,128]{1,0:T(8,128)S(1)} %broadcast_select_fusion), channel_id=1, source_target_pairs={{0,8},{16,24},{1,9},{17,25},{2,10},{18,26},{3,11},{19,27},{4,12},{... | collective-permute-start | bytes 442376 | tf_op jit(solution)/shard_map/ppermute | solution.py:459
  10.3 1.2 %copy-done.1 = f32[2,4,8,8,512]{4,3,2,1,0:T(8,128)S(1)} copy-done((f32[2,4,8,8,512]{4,3,2,1,0:T(8,128)S(1)}, f32[2,4,8,8,512]{4,3,2,1,0:T(8,128)}, u32[]{:S(2)}) %copy-start.1) | copy-done | bytes 1048600
  11.9 1.6 %collective-permute-start.2 = (f32[1024,128]{1,0:T(8,128)S(1)}, f32[1024,128]{1,0:T(8,128)S(1)}, u32[]{:S(2)}, u32[]{:S(2)}) collective-permute-start(f32[1024,128]{1,0:T(8,128)S(1)} %get-tuple-element.22.own), channel_id=1, source_target_pairs={{0,1},{1,0},{2,3},{3,2},{4,5},{5,4},{6,7},{7,6},{8,9},{9,8},{10,11... | collective-permute-start | bytes 1572872 | tf_op jit(solution)/shard_map/ppermute | solution.py:514
  13.8 1.3 %collective-permute-start = (f32[768,128]{1,0:T(8,128)S(1)}, f32[768,128]{1,0:T(8,128)S(1)}, u32[]{:S(2)}, u32[]{:S(2)}) collective-permute-start(f32[768,128]{1,0:T(8,128)S(1)} %get-tuple-element.23), channel_id=1, source_target_pairs={{0,4},{4,0},{1,5},{5,1},{2,6},{6,2},{3,7},{7,3},{8,12},{12,8},{9,1... | collective-permute-start | bytes 1179656 | tf_op jit(solution)/shard_map/ppermute | solution.py:503
  15.4 1.2 %collective-permute-start.1 = (f32[256,128]{1,0:T(8,128)S(1)}, f32[256,128]{1,0:T(8,128)S(1)}, u32[]{:S(2)}, u32[]{:S(2)}) collective-permute-start(f32[256,128]{1,0:T(8,128)S(1)} %get-tuple-element.24), channel_id=1, source_target_pairs={{0,4},{4,0},{1,5},{5,1},{2,6},{6,2},{3,7},{7,3},{8,12},{12,8},{9,1... | collective-permute-start | bytes 393224 | tf_op jit(solution)/shard_map/ppermute | solution.py:504
  16.6 13.8 %collective-permute-done.1.got_far = f32[256,128]{1,0:T(8,128)S(1)} collective-permute-done((f32[256,128]{1,0:T(8,128)S(1)}, f32[256,128]{1,0:T(8,128)S(1)}, u32[]{:S(2)}, u32[]{:S(2)}) %collective-permute-start.1) | collective-permute-done | bytes 131104 | tf_op jit(solution)/shard_map/ppermute | solution.py:504
  30.5 0.9 %collective-permute-start.4 = (f32[256,128]{1,0:T(8,128)S(1)}, f32[256,128]{1,0:T(8,128)S(1)}, u32[]{:S(2)}, u32[]{:S(2)}) collective-permute-start(f32[256,128]{1,0:T(8,128)S(1)} %collective-permute-done.1.got_far), channel_id=1, source_target_pairs={{0,1},{1,0},{2,3},{3,2},{4,5},{5,4},{6,7},{7,6},{8,9},{9,8},{10,11... | collective-permute-start | bytes 393224 | tf_op jit(solution)/shard_map/ppermute | solution.py:519
  31.4 3.0 %collective-permute-start.5 = (f32[768,128]{1,0:T(8,128)S(1)}, f32[768,128]{1,0:T(8,128)S(1)}, u32[]{:S(2)}, u32[]{:S(2)}) collective-permute-start(f32[768,128]{1,0:T(8,128)S(1)} %get-tuple-element.27), channel_id=1, source_target_pairs={{1,2},{2,1},{5,6},{6,5},{9,10},{10,9},{13,14},{14,13},{17,18},{18,... | collective-permute-start | bytes 1179656 | tf_op jit(solution)/shard_map/ppermute | solution.py:513
  34.5 2.5 %collective-permute-start.6 = (f32[768,128]{1,0:T(8,128)S(1)}, f32[768,128]{1,0:T(8,128)S(1)}, u32[]{:S(2)}, u32[]{:S(2)}) collective-permute-start(f32[768,128]{1,0:T(8,128)S(1)} %collective-permute-done.got_near), channel_id=1, source_target_pairs={{1,2},{2,1},{5,6},{6,5},{9,10},{10,9},{13,14},{14,13},{17,18},{18,... | collective-permute-start | bytes 1179656 | tf_op jit(solution)/shard_map/ppermute | solution.py:517
  37.1 3.0 %collective-permute-start.10 = (f32[576,128]{1,0:T(8,128)S(1)}, f32[576,128]{1,0:T(8,128)S(1)}, u32[]{:S(2)}, u32[]{:S(2)}) collective-permute-start(f32[576,128]{1,0:T(8,128)S(1)} %pad_maximum_fusion.p_own), channel_id=1, source_target_pairs={{1,2},{2,1},{5,6},{6,5},{9,10},{10,9},{13,14},{14,13},{17,18},{18,... | collective-permute-start | bytes 884744 | tf_op jit(solution)/shard_map/ppermute | solution.py:522
  42.2 0.7 weights.1
  43.1 2.3 %early.1 = (f32[11264,128]{1,0:T(8,128)S(1)}, f32[11264,128]{1,0:T(8,128)S(1)}) custom-call(f32[3,8,128]{2,1,0:T(8,128)S(1)} %get-tuple-element.20.trig, f32[2,2,4,2,8,128]{5,4,3,2,1,0:T(8,128)S(1)} %get-tuple-element.21.wgt, f32[11264,128]{1,0:T(8,128)S(1)} %fill.1.q_in, ...), custom_call_target="tpu_custom_call", output_to_operand_aliasing={{0}: (2, {})} | custom-call | tf_op jit(solution)/shard_map/early/pallas_call | solution.py:548
  45.4 4.2 %first.1 = (f32[11264,128]{1,0:T(8,128)S(1)}, f32[11264,128]{1,0:T(8,128)S(1)}) custom-call(f32[3,8,128]{2,1,0:T(8,128)S(1)} %get-tuple-element.20.trig, f32[2,2,4,2,8,128]{5,4,3,2,1,0:T(8,128)S(1)} %get-tuple-element.21.wgt, f32[11264,128]{1,0:T(8,128)S(1)} %get-tuple-element.25.q_in, ...), custom_call_target="tpu_custom_call", output_to_operand_aliasing={{0}: (2, {}), {1}: (3, {})} | custom-call | tf_op jit(solution)/shard_map/first/pallas_call | solution.py:558
  49.7 14.7 %rest.1 = (f32[512,128]{1,0:T(8,128)S(1)}, f32[11264,128]{1,0:T(8,128)S(1)}, f32[11264,128]{1,0:T(8,128)S(1)}, f32[5632,128]{1,0:T(8,128)S(1)}) custom-call(f32[3,8,128]{2,1,0:T(8,128)S(1)} %get-tuple-element.20.trig, f32[2,2,4,2,8,128]{5,4,3,2,1,0:T(8,128)S(1)} %get-tuple-element.21.wgt, ...), custom_call_target="tpu_custom_call", output_to_operand_aliasing={{1}: (2, {})} | custom-call | tf_op jit(solution)/shard_map/rest/pallas_call | solution.py:569
  64.3 1.3 %collective-permute-start.12 = (f32[512,128]{1,0:T(8,128)S(1)}, f32[512,128]{1,0:T(8,128)S(1)}, u32[]{:S(2)}, u32[]{:S(2)}) collective-permute-start(f32[512,128]{1,0:T(8,128)S(1)} %get-tuple-element.29), channel_id=1, source_target_pairs={{0,4},{4,0},{1,5},{5,1},{2,6},{6,2},{3,7},{7,3},{8,12},{12,8},{9,1... | collective-permute-start | bytes 786440 | tf_op jit(solution)/shard_map/ppermute | solution.py:579
  65.6 1.3 %upper.1 = (f32[512,128]{1,0:T(8,128)S(1)}, f32[11264,128]{1,0:T(8,128)S(1)}) custom-call(f32[3,8,128]{2,1,0:T(8,128)S(1)} %get-tuple-element.20.trig, f32[2,2,4,2,8,128]{5,4,3,2,1,0:T(8,128)S(1)} %get-tuple-element.21.wgt, f32[11264,128]{1,0:T(8,128)S(1)} %get-tuple-element.30.q, ...), custom_call_target="tpu_custom_call", output_to_operand_aliasing={{1}: (3, {})} | custom-call | tf_op jit(solution)/shard_map/upper/pallas_call | solution.py:580
  67.2 0.9 %last.1.refs_0_ = f32[1024,128]{1,0:T(8,128)S(1)} custom-call(f32[3,8,128]{2,1,0:T(8,128)S(1)} %get-tuple-element.20.trig, f32[2,2,4,2,8,128]{5,4,3,2,1,0:T(8,128)S(1)} %get-tuple-element.21.wgt, f32[11264,128]{1,0:T(8,128)S(1)} %get-tuple-element.30.q, f32[11264,128]{1,0:T(8,128)S(1)} %get-tuple-element.34.m, f32[5632,128]{1,0:T(8,128)S(1)} %get-tuple-element.32.pq), custom_call_target="tpu_custom_call" | custom-call | tf_op jit(solution)/shard_map/last/pallas_call | solution.py:591
  68.1 0.8 %place.2.refs_2_ = f32[2048,128]{1,0:T(8,128)} custom-call(f32[1024,128]{1,0:T(8,128)S(1)} %last.1.refs_0_), custom_call_target="tpu_custom_call" | custom-call | tf_op jit(solution)/shard_map/place/pallas_call | solution.py:603
  69.0 3.7 %collective-permute-done.12.refs_0_ = f32[512,128]{1,0:T(8,128)S(1)} collective-permute-done((f32[512,128]{1,0:T(8,128)S(1)}, f32[512,128]{1,0:T(8,128)S(1)}, u32[]{:S(2)}, u32[]{:S(2)}) %collective-permute-start.12) | collective-permute-done | bytes 262176 | tf_op jit(solution)/shard_map/ppermute | solution.py:579
  72.7 3.2 %collective-permute-done.13.refs_1_ = f32[512,128]{1,0:T(8,128)S(1)} collective-permute-done((f32[512,128]{1,0:T(8,128)S(1)}, f32[512,128]{1,0:T(8,128)S(1)}, u32[]{:S(2)}, u32[]{:S(2)}) %collective-permute-start.13) | collective-permute-done | bytes 262176 | tf_op jit(solution)/shard_map/ppermute | solution.py:590
  75.9 0.9 %place.3 = f32[2048,128]{1,0:T(8,128)} custom-call(f32[512,128]{1,0:T(8,128)S(1)} %collective-permute-done.12.refs_0_, f32[512,128]{1,0:T(8,128)S(1)} %collective-permute-done.13.refs_1_, f32[2048,128]{1,0:T(8,128)} %place.2.refs_2_), custom_call_target="tpu_custom_call", output_to_operand_aliasing={{}: (2, {})} | custom-call | tf_op jit(solution)/shard_map/place/pallas_call | solution.py:603
  (29 shorter events, 3.9 us)
Async XLA Ops:
  0.0 1.2 %copy-start = (f32[2,4,8,8,512]{4,3,2,1,0:T(8,128)S(1)}, f32[2,4,8,8,512]{4,3,2,1,0:T(8,128)}, u32[]{:S(2)}) copy-start(f32[2,4,8,8,512]{4,3,2,1,0:T(8,128)} %param.4) | copy-start | bytes 3145732
  1.4 7.6 %collective-permute-start.7 = (f32[288,128]{1,0:T(8,128)S(1)}, f32[288,128]{1,0:T(8,128)S(1)}, u32[]{:S(2)}, u32[]{:S(2)}) collective-permute-start(f32[288,128]{1,0:T(8,128)S(1)} %fringe.1), channel_id=1, source_target_pairs={{0,16},{1,17},{2,18},{3,19},{4,20},{5,21},{6,22},{7,23}} | collective-permute-start | bytes 442376 | tf_op jit(solution)/shard_map/ppermute | solution.py:459
  9.0 6.1 %collective-permute-start.8 = (f32[288,128]{1,0:T(8,128)S(1)}, f32[288,128]{1,0:T(8,128)S(1)}, u32[]{:S(2)}, u32[]{:S(2)}) collective-permute-start(f32[288,128]{1,0:T(8,128)S(1)} %broadcast_select_fusion), channel_id=1, source_target_pairs={{0,8},{16,24},{1,9},{17,25},{2,10},{18,26},{3,11},{19,27},{4,12},{... | collective-permute-start | bytes 442376 | tf_op jit(solution)/shard_map/ppermute | solution.py:459
  10.3 1.2 %copy-start.1 = (f32[2,4,8,8,512]{4,3,2,1,0:T(8,128)S(1)}, f32[2,4,8,8,512]{4,3,2,1,0:T(8,128)}, u32[]{:S(2)}) copy-start(f32[2,4,8,8,512]{4,3,2,1,0:T(8,128)} %param.4) | copy-start | bytes 3145732
  11.9 28.2 %collective-permute-start.2 = (f32[1024,128]{1,0:T(8,128)S(1)}, f32[1024,128]{1,0:T(8,128)S(1)}, u32[]{:S(2)}, u32[]{:S(2)}) collective-permute-start(f32[1024,128]{1,0:T(8,128)S(1)} %get-tuple-element.22.own), channel_id=1, source_target_pairs={{0,1},{1,0},{2,3},{3,2},{4,5},{5,4},{6,7},{7,6},{8,9},{9,8},{10,11... | collective-permute-start | bytes 1572872 | tf_op jit(solution)/shard_map/ppermute | solution.py:514
  13.8 20.6 %collective-permute-start = (f32[768,128]{1,0:T(8,128)S(1)}, f32[768,128]{1,0:T(8,128)S(1)}, u32[]{:S(2)}, u32[]{:S(2)}) collective-permute-start(f32[768,128]{1,0:T(8,128)S(1)} %get-tuple-element.23), channel_id=1, source_target_pairs={{0,4},{4,0},{1,5},{5,1},{2,6},{6,2},{3,7},{7,3},{8,12},{12,8},{9,1... | collective-permute-start | bytes 1179656 | tf_op jit(solution)/shard_map/ppermute | solution.py:503
  15.1 19.4 %collective-permute-start.9 = (f32[288,128]{1,0:T(8,128)S(1)}, f32[288,128]{1,0:T(8,128)S(1)}, u32[]{:S(2)}, u32[]{:S(2)}) collective-permute-start(f32[288,128]{1,0:T(8,128)S(1)} %broadcast_select_fusion.1), channel_id=1, source_target_pairs={{0,4},{4,0},{1,5},{5,1},{2,6},{6,2},{3,7},{7,3},{8,12},{12,8},{9,1... | collective-permute-start | bytes 442376 | tf_op jit(solution)/shard_map/ppermute | solution.py:516
  15.4 15.0 %collective-permute-start.1 = (f32[256,128]{1,0:T(8,128)S(1)}, f32[256,128]{1,0:T(8,128)S(1)}, u32[]{:S(2)}, u32[]{:S(2)}) collective-permute-start(f32[256,128]{1,0:T(8,128)S(1)} %get-tuple-element.24), channel_id=1, source_target_pairs={{0,4},{4,0},{1,5},{5,1},{2,6},{6,2},{3,7},{7,3},{8,12},{12,8},{9,1... | collective-permute-start | bytes 393224 | tf_op jit(solution)/shard_map/ppermute | solution.py:504
  30.5 6.6 %collective-permute-start.4 = (f32[256,128]{1,0:T(8,128)S(1)}, f32[256,128]{1,0:T(8,128)S(1)}, u32[]{:S(2)}, u32[]{:S(2)}) collective-permute-start(f32[256,128]{1,0:T(8,128)S(1)} %collective-permute-done.1.got_far), channel_id=1, source_target_pairs={{0,1},{1,0},{2,3},{3,2},{4,5},{5,4},{6,7},{7,6},{8,9},{9,8},{10,11... | collective-permute-start | bytes 393224 | tf_op jit(solution)/shard_map/ppermute | solution.py:519
  31.4 14.0 %collective-permute-start.5 = (f32[768,128]{1,0:T(8,128)S(1)}, f32[768,128]{1,0:T(8,128)S(1)}, u32[]{:S(2)}, u32[]{:S(2)}) collective-permute-start(f32[768,128]{1,0:T(8,128)S(1)} %get-tuple-element.27), channel_id=1, source_target_pairs={{1,2},{2,1},{5,6},{6,5},{9,10},{10,9},{13,14},{14,13},{17,18},{18,... | collective-permute-start | bytes 1179656 | tf_op jit(solution)/shard_map/ppermute | solution.py:513
  34.4 8.7 %collective-permute-start.3 = (f32[768,128]{1,0:T(8,128)S(1)}, f32[768,128]{1,0:T(8,128)S(1)}, u32[]{:S(2)}, u32[]{:S(2)}) collective-permute-start(f32[768,128]{1,0:T(8,128)S(1)} %collective-permute-done.got_near), channel_id=1, source_target_pairs={{0,1},{1,0},{2,3},{3,2},{4,5},{5,4},{6,7},{7,6},{8,9},{9,8},{10,11... | collective-permute-start | bytes 1179656 | tf_op jit(solution)/shard_map/ppermute | solution.py:518
  34.5 10.9 %collective-permute-start.6 = (f32[768,128]{1,0:T(8,128)S(1)}, f32[768,128]{1,0:T(8,128)S(1)}, u32[]{:S(2)}, u32[]{:S(2)}) collective-permute-start(f32[768,128]{1,0:T(8,128)S(1)} %collective-permute-done.got_near), channel_id=1, source_target_pairs={{1,2},{2,1},{5,6},{6,5},{9,10},{10,9},{13,14},{14,13},{17,18},{18,... | collective-permute-start | bytes 1179656 | tf_op jit(solution)/shard_map/ppermute | solution.py:517
  37.1 12.6 %collective-permute-start.10 = (f32[576,128]{1,0:T(8,128)S(1)}, f32[576,128]{1,0:T(8,128)S(1)}, u32[]{:S(2)}, u32[]{:S(2)}) collective-permute-start(f32[576,128]{1,0:T(8,128)S(1)} %pad_maximum_fusion.p_own), channel_id=1, source_target_pairs={{1,2},{2,1},{5,6},{6,5},{9,10},{10,9},{13,14},{14,13},{17,18},{18,... | collective-permute-start | bytes 884744 | tf_op jit(solution)/shard_map/ppermute | solution.py:522
  40.1 9.5 %collective-permute-start.11 = (f32[576,128]{1,0:T(8,128)S(1)}, f32[576,128]{1,0:T(8,128)S(1)}, u32[]{:S(2)}, u32[]{:S(2)}) collective-permute-start(f32[576,128]{1,0:T(8,128)S(1)} %pad_maximum_fusion.p_own), channel_id=1, source_target_pairs={{0,1},{1,0},{2,3},{3,2},{4,5},{5,4},{6,7},{7,6},{8,9},{9,8},{10,11... | collective-permute-start | bytes 884744 | tf_op jit(solution)/shard_map/ppermute | solution.py:522
  40.2 0.7 copy-start.2
  40.9 0.7 copy-start.3
  41.6 0.7 copy-start.4
  64.3 8.4 %collective-permute-start.12 = (f32[512,128]{1,0:T(8,128)S(1)}, f32[512,128]{1,0:T(8,128)S(1)}, u32[]{:S(2)}, u32[]{:S(2)}) collective-permute-start(f32[512,128]{1,0:T(8,128)S(1)} %get-tuple-element.29), channel_id=1, source_target_pairs={{0,4},{4,0},{1,5},{5,1},{2,6},{6,2},{3,7},{7,3},{8,12},{12,8},{9,1... | collective-permute-start | bytes 786440 | tf_op jit(solution)/shard_map/ppermute | solution.py:579
  66.9 9.0 %collective-permute-start.13 = (f32[512,128]{1,0:T(8,128)S(1)}, f32[512,128]{1,0:T(8,128)S(1)}, u32[]{:S(2)}, u32[]{:S(2)}) collective-permute-start(f32[512,128]{1,0:T(8,128)S(1)} %get-tuple-element.33), channel_id=1, source_target_pairs={{0,4},{4,0},{1,5},{5,1},{2,6},{6,2},{3,7},{7,3},{8,12},{12,8},{9,1... | collective-permute-start | bytes 786440 | tf_op jit(solution)/shard_map/ppermute | solution.py:590
